TPU v7x, 256 devices: a whole 4x4x8 slice. The times are simulated.
256 devices in a mesh: strip: 4 (over x), lvl: 64 (over z, y, core).
Axes of the slice: x: 4, y: 4, z: 8, core: 2. Of those that a mesh axis runs over, the one named last changes fastest.
Arguments:
- photos: bfloat16 [16, 3, 64, 65536], P('strip', None, None, 'lvl'), may hold values from -6 to 6
- seams: int32 [16, 2, 64], P('strip'), may hold values from 0 to 65536, as said below
- offsets: int32 [16], P('strip'), may hold values from 0 to 2, as said below
Outputs:
- blended: float32 [3, 128, 65536], P(None, 'strip', 'lvl')
Inputs may be any that keep to these rules, and one draw needn't show every extreme that they name: offsets[p] differs from p // 4 by at most 2; every strip is the first or the second strip of some photo. seams[p, 0, r] <= seams[p, 1, r]; in each panorama row the intervals of the photos that cover it are disjoint and together cover all 65536 columns.
All inputs are finite; a program needn't handle non-finite values.
Results may differ from a plain program's by a relative error of at most 0.003.
Values may be sent and summed in bfloat16 or wider, within the bound.
A program may use at most 64 MiB of HBM per device.

v0:
```python
import jax
import jax.numpy as jnp
from jax import lax
from jax.sharding import PartitionSpec as P

LEVELS = 6


TAPS = (0.0625, 0.25, 0.375, 0.25, 0.0625)
highest = lax.Precision.HIGHEST


def extended(x, sides, width):
    for axis, dim in sides:
        size, length = (lax.axis_size(axis), x.shape[dim])
        up = [(i, (i + 1) % size) for i in range(size - 1)]
        down = [(j, i) for i, j in up]
        last = lax.slice_in_dim(x, length - width, length, axis=dim)
        initial = lax.slice_in_dim(x, 0, width, axis=dim)
        before = lax.ppermute(last, axis, up)
        after = lax.ppermute(initial, axis, down)
        x = jnp.concatenate([before, x, after], axis=dim)
    return x


def for_sending(x):

    def short(part):
        return part.astype(jnp.bfloat16) if part.dtype == jnp.float32 else part

    return jax.tree.map(short, x)


def reduce_table(length_in, count_out, shift_by):
    distance = (
        jnp.arange(length_in, dtype=jnp.int32)[:, None]
        + shift_by
        - 2 * jnp.arange(count_out, dtype=jnp.int32)[None, :]
    )
    matrix = jnp.zeros((length_in, count_out), jnp.float32)
    for which in range(5):
        matrix = matrix + jnp.where(distance == which, TAPS[which], 0.0).astype(jnp.float32)
    return matrix


def expand_table(length_in, count_out, shift_by):
    target = jnp.arange(count_out, dtype=jnp.int32)[None, :]
    distance = jnp.arange(length_in, dtype=jnp.int32)[:, None] + shift_by - target // 2
    even_weight = jnp.where(
        distance == 1, 0.75, jnp.where((distance == 0) | (distance == 2), 0.125, 0.0)
    )
    odd_weight = jnp.where((distance == 1) | (distance == 2), 0.5, 0.0)
    return jnp.where(target % 2 == 0, even_weight, odd_weight).astype(jnp.float32)


def apply_columns(field, matrix):
    return jnp.matmul(field, matrix, precision=highest)


def apply_rows(field, matrix):
    return jnp.einsum("...rw,rs->...sw", field, matrix, precision=highest)


def photo_pad(field, width):
    return extended(field, (("lvl", 3),), width)


def photo_reduce(field):
    rows = field.shape[2]
    cols = field.shape[3]
    wide = photo_pad(field, 2)
    across = apply_columns(wide, reduce_table(cols + 4, cols // 2, 0))
    return apply_rows(across, reduce_table(rows, rows // 2, 2))


def photo_expand(field):
    rows = field.shape[2]
    cols = field.shape[3]
    wide = photo_pad(field, 1)
    across = apply_columns(wide, expand_table(cols + 2, 2 * cols, 0))
    return apply_rows(across, expand_table(rows, 2 * rows, 1))


def band_expand(field):
    rows = field.shape[1]
    cols = field.shape[2]
    padded = extended(field, (("strip", 1), ("lvl", 2)), 1)
    across = apply_columns(padded, expand_table(cols + 2, 2 * cols, 0))
    return apply_rows(across, expand_table(rows + 2, 2 * rows, 0))


def gather_blocks(weighted, targets, slots):
    count, channels, tall, width = weighted.shape
    half = tall // 2
    blocks = weighted.reshape(count, channels, 2, half, width).transpose(0, 2, 1, 3, 4)
    blocks = blocks.reshape(2 * count, channels, half, width).astype(jnp.float32)
    buffer = jnp.zeros((slots, channels, half, width), jnp.float32)
    return buffer.at[targets].add(blocks).astype(jnp.bfloat16)


def per_device(photos, seams, offsets):
    count, channels, tall, width = photos.shape
    column = lax.axis_index("lvl") * width + jnp.arange(width, dtype=jnp.int32)
    mask = (
        (column[None, None, :] >= seams[:, 0, :, None])
        & (column[None, None, :] < seams[:, 1, :, None])
    ).astype(jnp.float32)
    level = jnp.concatenate([photos.astype(jnp.float32), mask[:, None]], axis=1)
    gauss = [level]
    for step in range(LEVELS - 1):
        gauss.append(photo_reduce(gauss[-1]))
    weighted = []
    for step in range(LEVELS):
        detail = gauss[step][:, :channels]
        if step + 1 < LEVELS:
            detail = detail - photo_expand(gauss[step + 1][:, :channels])
        weighted.append((gauss[step][:, channels:] * detail).astype(jnp.bfloat16))
    targets = (offsets[:, None] + jnp.arange(2, dtype=jnp.int32)[None, :]).reshape(-1)
    strips = lax.axis_size("strip")
    parts = tuple((gather_blocks(weighted[step], targets, strips) for step in range(LEVELS)))
    received = jax.tree.map(
        lambda part, own: part.astype(own.dtype),
        lax.all_to_all(for_sending(parts), "strip", split_axis=0, concat_axis=0, tiled=True),
        parts,
    )
    bands = [jnp.sum(piece, axis=0, dtype=jnp.float32) for piece in received]
    total = bands[LEVELS - 1]
    for step in range(LEVELS - 2, -1, -1):
        total = bands[step] + band_expand(total)
    return total


def solution(mesh):
    placed = (P("strip", None, None, "lvl"), P("strip", None, None), P("strip"))
    return jax.shard_map(
        per_device, mesh=mesh, in_specs=placed, out_specs=P(None, "strip", "lvl"), check_vma=False
    )
```

profile of v0, /device:TPU:121, one launch (start us, length us, event | category | flops | bytes accessed | tf_op | source)
XLA Modules:
  0.0 281.1 jit_solution(16002904493400403045)
XLA Ops:
  3.0 5.0 %collective-permute-start = (f32[4,4,64,2]{3,2,1,0:T(8,128)S(1)}, f32[4,4,64,2]{3,2,1,0:T(8,128)S(1)}, u32[]{:S(2)}, u32[]{:S(2)}) collective-permute-start(f32[4,4,64,2]{3,2,1,0:T(8,128)S(1)} %get-tuple-element.6), channel_id=1, source_target_pairs={{0,1},{1,2},{2,3},{3,4},{4,5},{5,6},{6,7},{7,8},{8,9},{9,10},{10,1... | collective-permute-start | bytes 24584 | tf_op jit(solution)/shard_map/ppermute | solution.py:20
  9.9 2.4 pad_maximum_fusion
  14.1 7.7 %collective-permute-done.1 = f32[4,4,64,2]{3,2,1,0:T(8,128)S(1)} collective-permute-done((f32[4,4,64,2]{3,2,1,0:T(8,128)S(1)}, f32[4,4,64,2]{3,2,1,0:T(8,128)S(1)}, u32[]{:S(2)}, u32[]{:S(2)}) %collective-permute-start.1) | collective-permute-done | bytes 8224 | tf_op jit(solution)/shard_map/ppermute | solution.py:21
  21.8 6.4 %concatenate.79 = f32[4,4,64,1028]{3,2,1,0:T(8,128)} concatenate(f32[4,4,64,2]{3,2,1,0:T(8,128)S(1)} %collective-permute-done, f32[4,4,64,1024]{3,2,1,0:T(8,128)} %pad_maximum_fusion, f32[4,4,64,2]{3,2,1,0:T(8,128)S(1)} %collective-permute-done.1), dimensions={3} | concatenate | bytes 8421376 | tf_op jit(solution)/shard_map/concatenate | solution.py:22
  28.2 13.4 %fusion.11 = f32[4,4,64,512]{3,2,1,0:T(8,128)S(1)} fusion(f32[4,4,64,1028]{3,2,1,0:T(8,128)} %concatenate.79, s32[512]{0:T(512)S(1)} %iota_multiply_fusion), kind=kOutput, calls=%fused_computation.25 | convolution fusion | flops 6475511808 | bytes 6309888 | tf_op jit(solution)/shard_map/dot_general | solution.py:57
  44.9 2.4 collective-permute-start.3
  47.4 6.5 %collective-permute-start.4 = (f32[4,4,32,2]{3,2,1,0:T(8,128)S(1)}, f32[4,4,32,2]{3,2,1,0:T(8,128)}, u32[]{:S(2)}, u32[]{:S(2)}) collective-permute-start(f32[4,4,32,2]{3,2,1,0:T(8,128)S(1)} %get-tuple-element.9), channel_id=1, source_target_pairs={{0,1},{1,2},{2,3},{3,4},{4,5},{5,6},{6,7},{7,8},{8,9},{9,10},{10,1... | collective-permute-start | bytes 12296 | tf_op jit(solution)/shard_map/ppermute | solution.py:20
  53.9 2.2 collective-permute-start.5
  56.2 4.8 %fusion.2 = f32[4,3,32,1024]{3,2,1,0:T(8,128)S(1)} fusion(s32[1024]{0:T(1024)S(1)} %add_select_fusion, pred[1024]{0:T(1024)(128)(4,1)S(1)} %fusion.506, f32[4,3,32,1]{3,2,1,0:T(8,128)S(1)} %collective-permute-done.3, f32[4,3,32,512]{3,2,1,0:T(8,128)S(1)} %slice.260, f32[4,3,32,1]{3,2,1,0:T(8,128)S(1)} %collective-permute-done.2), kind=kOutput, calls=%fused_computation.14 | convolution fusion | flops 2431014400 | bytes 2367488 | tf_op jit(solution)/shard_map/dot_general | solution.py:57
  61.1 3.0 %fusion.1 = bf16[4,3,64,1024]{3,2,1,0:T(8,128)(2,1)S(1)} fusion(f32[4,3,32,1024]{3,2,1,0:T(8,128)S(1)} %fusion.2, f32[4,64,1024]{2,1,0:T(8,128)S(1)} %and_convert_fusion.1, bf16[4,3,64,1024]{3,2,1,0:T(8,128)(2,1)S(1)} %copy-done, s32[64]{0:T(128)S(1)} %and_select_fusion.14, s32[32]{0:T(128)S(1)} %iota_add_fusion.11, pred[64]{0:T(512)(128)(4,1)S(1)} %fusion.692), kind=kOutput, calls=%fused_computation.13 | convolution fusion | flops 305156096 | bytes 5767616 | tf_op jit(solution)/shard_map/...rw,rs->...sw/dot_general | solution.py:61
  66.6 4.9 %scatter_fusion = f32[4,3,32,1024]{3,2,1,0:T(8,128)S(1)} fusion(f32[4,3,32,1024]{3,2,1,0:T(8,128)S(1)} %broadcast_in_dim.699, s32[8]{0:T(128)S(1)} %fusion.699, f32[8,3,32,1024]{3,2,1,0:T(8,128)} %convert.8), kind=kCustom, calls=%fused_computation | custom fusion | flops 786432 | bytes 9437216 | tf_op jit(solution)/shard_map/scatter-add | solution.py:98
  72.6 2.7 fusion.32
  75.9 7.0 %collective-permute-start.6 = (f32[4,3,16,1]{3,2,1,0:T(8,128)S(1)}, f32[4,3,16,1]{3,2,1,0:T(8,128)S(1)}, u32[]{:S(2)}, u32[]{:S(2)}) collective-permute-start(f32[4,3,16,1]{3,2,1,0:T(8,128)S(1)} %get-tuple-element.17), channel_id=1, source_target_pairs={{0,1},{1,2},{2,3},{3,4},{4,5},{5,6},{6,7},{7,8},{8,9},{9,10},{10,1... | collective-permute-start | bytes 2312 | tf_op jit(solution)/shard_map/ppermute | solution.py:20
  84.9 7.0 %collective-permute-start.8 = (f32[4,4,16,2]{3,2,1,0:T(8,128)S(1)}, f32[4,4,16,2]{3,2,1,0:T(8,128)S(1)}, u32[]{:S(2)}, u32[]{:S(2)}) collective-permute-start(f32[4,4,16,2]{3,2,1,0:T(8,128)S(1)} %get-tuple-element.15), channel_id=1, source_target_pairs={{0,1},{1,2},{2,3},{3,4},{4,5},{5,6},{6,7},{7,8},{8,9},{9,10},{10,1... | collective-permute-start | bytes 6152 | tf_op jit(solution)/shard_map/ppermute | solution.py:20
  96.1 5.4 %collective-permute-done.9 = f32[4,4,16,2]{3,2,1,0:T(8,128)S(1)} collective-permute-done((f32[4,4,16,2]{3,2,1,0:T(8,128)S(1)}, f32[4,4,16,2]{3,2,1,0:T(8,128)S(1)}, u32[]{:S(2)}, u32[]{:S(2)}) %collective-permute-start.9) | collective-permute-done | bytes 2080 | tf_op jit(solution)/shard_map/ppermute | solution.py:21
  104.4 2.4 collective-permute-start.11
  106.8 6.5 %collective-permute-start.12 = (f32[4,4,8,2]{3,2,1,0:T(8,128)S(1)}, f32[4,4,8,2]{3,2,1,0:T(8,128)S(1)}, u32[]{:S(2)}, u32[]{:S(2)}) collective-permute-start(f32[4,4,8,2]{3,2,1,0:T(8,128)S(1)} %get-tuple-element.25), channel_id=1, source_target_pairs={{0,1},{1,2},{2,3},{3,4},{4,5},{5,6},{6,7},{7,8},{8,9},{9,10},{10,1... | collective-permute-start | bytes 3080 | tf_op jit(solution)/shard_map/ppermute | solution.py:20
  116.1 6.2 %collective-permute-done.13 = f32[4,4,8,2]{3,2,1,0:T(8,128)S(1)} collective-permute-done((f32[4,4,8,2]{3,2,1,0:T(8,128)S(1)}, f32[4,4,8,2]{3,2,1,0:T(8,128)S(1)}, u32[]{:S(2)}, u32[]{:S(2)}) %collective-permute-start.13) | collective-permute-done | bytes 1056 | tf_op jit(solution)/shard_map/ppermute | solution.py:21
  126.9 2.4 collective-permute-start.15
  129.3 3.6 %collective-permute-start.17 = (f32[4,4,4,2]{3,2,1,0:T(4,128)S(1)}, f32[4,4,4,2]{3,2,1,0:T(4,128)S(1)}, u32[]{:S(2)}, u32[]{:S(2)}) collective-permute-start(f32[4,4,4,2]{3,2,1,0:T(4,128)S(1)} %get-tuple-element.32), channel_id=1, source_target_pairs={{1,0},{2,1},{3,2},{4,3},{5,4},{6,5},{7,6},{8,7},{9,8},{10,9},{11,1... | collective-permute-start | bytes 1544 | tf_op jit(solution)/shard_map/ppermute | solution.py:21
  133.0 2.4 collective-permute-done.15
  139.9 4.0 %all-to-all-start.5 = ((bf16[4,3,1,32]{3,1,2,0:T(4,128)(2,1)}), bf16[4,3,1,32]{3,1,2,0:T(4,128)(2,1)S(1)}, u32[]{:S(2)}, u32[]{:S(2)}) async-start(bf16[4,3,1,32]{3,1,2,0:T(4,128)(2,1)} %convert_bitcast_fusion.1), calls=%async_computation.5 | async-start | bytes 8192 | tf_op jit(solution)/shard_map/all_to_all | solution.py:123
  144.0 2.2 collective-permute-start.18
  148.3 6.2 %collective-permute-done.19 = f32[4,3,2,1]{3,2,1,0:T(2,128)S(1)} collective-permute-done((f32[4,3,2,1]{3,2,1,0:T(2,128)S(1)}, f32[4,3,2,1]{3,2,1,0:T(2,128)S(1)}, u32[]{:S(2)}, u32[]{:S(2)}) %collective-permute-start.19) | collective-permute-done | bytes 128 | tf_op jit(solution)/shard_map/ppermute | solution.py:21
  155.2 3.7 %collective-permute-start.20 = (f32[3,1,32]{2,1,0:T(1,128)S(1)}, f32[3,1,32]{2,1,0:T(1,128)S(1)}, u32[]{:S(2)}, u32[]{:S(2)}) collective-permute-start(f32[3,1,32]{2,1,0:T(1,128)S(1)} %copy.41), channel_id=1, source_target_pairs={{0,64},{64,128},{128,192},{1,65},{65,129},{129,193},{2,66},{66,130... | collective-permute-start | bytes 1160 | tf_op jit(solution)/shard_map/ppermute | solution.py:20
  161.7 4.9 %all-to-all-start.4 = ((bf16[4,2,192]{2,1,0:T(2,128)(2,1)}), bf16[4,2,192]{2,1,0:T(2,128)(2,1)S(1)}, u32[]{:S(2)}, u32[]{:S(2)}) async-start(bf16[4,2,192]{2,1,0:T(2,128)(2,1)} %reshape.812), calls=%async_computation.4 | async-start | bytes 8192 | tf_op jit(solution)/shard_map/all_to_all | solution.py:123
  166.6 2.8 collective-permute-start.22
  171.4 6.3 %collective-permute-done.23 = f32[3,3,1]{2,1,0:T(4,128)S(1)} collective-permute-done((f32[3,3,1]{2,1,0:T(4,128)S(1)}, f32[3,3,1]{2,1,0:T(4,128)S(1)}, u32[]{:S(2)}, u32[]{:S(2)}) %collective-permute-start.23) | collective-permute-done | bytes 68 | tf_op jit(solution)/shard_map/ppermute | solution.py:21
  178.3 3.6 %collective-permute-start.24 = (f32[3,1,64]{2,1,0:T(1,128)S(1)}, f32[3,1,64]{2,1,0:T(1,128)S(1)}, u32[]{:S(2)}, u32[]{:S(2)}) collective-permute-start(f32[3,1,64]{2,1,0:T(1,128)S(1)} %get-tuple-element.55), channel_id=1, source_target_pairs={{0,64},{64,128},{128,192},{1,65},{65,129},{129,193},{2,66},{66,130... | collective-permute-start | bytes 2312 | tf_op jit(solution)/shard_map/ppermute | solution.py:20
  184.7 4.9 %all-to-all-start.3 = ((bf16[4,3,4,128]{3,2,1,0:T(4,128)(2,1)}), bf16[4,3,4,128]{3,2,1,0:T(4,128)(2,1)S(1)}, u32[]{:S(2)}, u32[]{:S(2)}) async-start(bf16[4,3,4,128]{3,2,1,0:T(4,128)(2,1)} %convert_element_type.141), calls=%async_computation.3 | async-start | bytes 24576 | tf_op jit(solution)/shard_map/all_to_all | solution.py:123
  189.7 2.8 collective-permute-start.26
  194.4 6.3 %collective-permute-done.27 = f32[3,4,1]{2,1,0:T(4,128)S(1)} collective-permute-done((f32[3,4,1]{2,1,0:T(4,128)S(1)}, f32[3,4,1]{2,1,0:T(4,128)S(1)}, u32[]{:S(2)}, u32[]{:S(2)}) %collective-permute-start.27) | collective-permute-done | bytes 80 | tf_op jit(solution)/shard_map/ppermute | solution.py:21
  201.2 3.6 %collective-permute-start.28 = (f32[3,1,128]{2,1,0:T(1,128)S(1)}, f32[3,1,128]{2,1,0:T(1,128)S(1)}, u32[]{:S(2)}, u32[]{:S(2)}) collective-permute-start(f32[3,1,128]{2,1,0:T(1,128)S(1)} %get-tuple-element.47), channel_id=1, source_target_pairs={{0,64},{64,128},{128,192},{1,65},{65,129},{129,193},{2,66},{66,130... | collective-permute-start | bytes 4616 | tf_op jit(solution)/shard_map/ppermute | solution.py:20
  207.7 4.9 %all-to-all-start.2 = ((bf16[4,3,8,256]{3,2,1,0:T(8,128)(2,1)}), bf16[4,3,8,256]{3,2,1,0:T(8,128)(2,1)S(1)}, u32[]{:S(2)}, u32[]{:S(2)}) async-start(bf16[4,3,8,256]{3,2,1,0:T(8,128)(2,1)} %convert_element_type.136), calls=%async_computation.2 | async-start | bytes 98304 | tf_op jit(solution)/shard_map/all_to_all | solution.py:123
  212.7 2.8 collective-permute-start.30
  217.4 6.4 %collective-permute-done.31 = f32[3,6,1]{2,1,0:T(8,128)S(1)} collective-permute-done((f32[3,6,1]{2,1,0:T(8,128)S(1)}, f32[3,6,1]{2,1,0:T(8,128)S(1)}, u32[]{:S(2)}, u32[]{:S(2)}) %collective-permute-start.31) | collective-permute-done | bytes 104 | tf_op jit(solution)/shard_map/ppermute | solution.py:21
  224.4 3.6 %collective-permute-start.32 = (f32[3,1,256]{2,1,0:T(1,128)S(1)}, f32[3,1,256]{2,1,0:T(1,128)S(1)}, u32[]{:S(2)}, u32[]{:S(2)}) collective-permute-start(f32[3,1,256]{2,1,0:T(1,128)S(1)} %get-tuple-element.35), channel_id=1, source_target_pairs={{0,64},{64,128},{128,192},{1,65},{65,129},{129,193},{2,66},{66,130... | collective-permute-start | bytes 9224 | tf_op jit(solution)/shard_map/ppermute | solution.py:20
  232.5 3.4 %collective-permute-start.34 = (f32[3,10,1]{2,1,0:T(8,128)S(1)}, f32[3,10,1]{2,1,0:T(8,128)S(1)}, u32[]{:S(2)}, u32[]{:S(2)}) collective-permute-start(f32[3,10,1]{2,1,0:T(8,128)S(1)} %get-tuple-element.29), channel_id=1, source_target_pairs={{0,1},{1,2},{2,3},{3,4},{4,5},{5,6},{6,7},{7,8},{8,9},{9,10},{10,1... | collective-permute-start | bytes 368 | tf_op jit(solution)/shard_map/ppermute | solution.py:20
  237.8 3.7 %all-to-all-start.1 = ((bf16[4,3,16,512]{3,2,1,0:T(8,128)(2,1)}), bf16[4,3,16,512]{3,2,1,0:T(8,128)(2,1)S(1)}, u32[]{:S(2)}, u32[]{:S(2)}) async-start(bf16[4,3,16,512]{3,2,1,0:T(8,128)(2,1)} %convert_element_type.131), calls=%async_computation.1 | async-start | bytes 393216 | tf_op jit(solution)/shard_map/all_to_all | solution.py:123
  241.5 2.9 %collective-permute-done.35 = f32[3,10,1]{2,1,0:T(8,128)S(1)} collective-permute-done((f32[3,10,1]{2,1,0:T(8,128)S(1)}, f32[3,10,1]{2,1,0:T(8,128)S(1)}, u32[]{:S(2)}, u32[]{:S(2)}) %collective-permute-start.35) | collective-permute-done | bytes 152 | tf_op jit(solution)/shard_map/ppermute | solution.py:21
  245.1 2.9 %all-to-all-done.1 = bf16[4,3,16,512]{3,2,1,0:T(8,128)(2,1)S(1)} async-done(((bf16[4,3,16,512]{3,2,1,0:T(8,128)(2,1)}), bf16[4,3,16,512]{3,2,1,0:T(8,128)(2,1)S(1)}, u32[]{:S(2)}, u32[]{:S(2)}) %all-to-all-start.1) | async-done | bytes 196640 | tf_op jit(solution)/shard_map/all_to_all | solution.py:123
  247.9 3.5 %all-to-all-start = ((bf16[4,3,32,1024]{3,2,1,0:T(8,128)(2,1)}), bf16[4,3,32,1024]{3,2,1,0:T(8,128)(2,1)S(1)}, u32[]{:S(2)}, u32[]{:S(2)}) async-start(bf16[4,3,32,1024]{3,2,1,0:T(8,128)(2,1)} %convert_element_type.126), calls=%async_computation | async-start | bytes 1572864 | tf_op jit(solution)/shard_map/all_to_all | solution.py:123
  251.8 3.3 %collective-permute-start.36 = (f32[3,1,512]{2,1,0:T(1,128)S(1)}, f32[3,1,512]{2,1,0:T(1,128)S(1)}, u32[]{:S(2)}, u32[]{:S(2)}) collective-permute-start(f32[3,1,512]{2,1,0:T(1,128)S(1)} %get-tuple-element.21), channel_id=1, source_target_pairs={{0,64},{64,128},{128,192},{1,65},{65,129},{129,193},{2,66},{66,130... | collective-permute-start | bytes 18440 | tf_op jit(solution)/shard_map/ppermute | solution.py:20
  256.4 3.7 %collective-permute-done.36 = f32[3,1,512]{2,1,0:T(1,128)S(1)} collective-permute-done((f32[3,1,512]{2,1,0:T(1,128)S(1)}, f32[3,1,512]{2,1,0:T(1,128)S(1)}, u32[]{:S(2)}, u32[]{:S(2)}) %collective-permute-start.36) | collective-permute-done | bytes 6176 | tf_op jit(solution)/shard_map/ppermute | solution.py:20
  262.1 6.3 %collective-permute-start.38 = (f32[3,18,1]{2,1,0:T(8,128)S(1)}, f32[3,18,1]{2,1,0:T(8,128)S(1)}, u32[]{:S(2)}, u32[]{:S(2)}) collective-permute-start(f32[3,18,1]{2,1,0:T(8,128)S(1)} %get-tuple-element.19), channel_id=1, source_target_pairs={{0,1},{1,2},{2,3},{3,4},{4,5},{5,6},{6,7},{7,8},{8,9},{9,10},{10,1... | collective-permute-start | bytes 656 | tf_op jit(solution)/shard_map/ppermute | solution.py:20
  268.4 2.2 collective-permute-start.39
  270.6 6.4 %collective-permute-done.39 = f32[3,18,1]{2,1,0:T(8,128)S(1)} collective-permute-done((f32[3,18,1]{2,1,0:T(8,128)S(1)}, f32[3,18,1]{2,1,0:T(8,128)S(1)}, u32[]{:S(2)}, u32[]{:S(2)}) %collective-permute-start.39) | collective-permute-done | bytes 248 | tf_op jit(solution)/shard_map/ppermute | solution.py:21
  277.0 2.7 fusion.4
  (208 shorter events, 65.8 us)
Async XLA Ops:
  3.0 11.1 %collective-permute-start = (f32[4,4,64,2]{3,2,1,0:T(8,128)S(1)}, f32[4,4,64,2]{3,2,1,0:T(8,128)S(1)}, u32[]{:S(2)}, u32[]{:S(2)}) collective-permute-start(f32[4,4,64,2]{3,2,1,0:T(8,128)S(1)} %get-tuple-element.6), channel_id=1, source_target_pairs={{0,1},{1,2},{2,3},{3,4},{4,5},{5,6},{6,7},{7,8},{8,9},{9,10},{10,1... | collective-permute-start | bytes 24584 | tf_op jit(solution)/shard_map/ppermute | solution.py:20
  8.0 13.8 %collective-permute-start.1 = (f32[4,4,64,2]{3,2,1,0:T(8,128)S(1)}, f32[4,4,64,2]{3,2,1,0:T(8,128)S(1)}, u32[]{:S(2)}, u32[]{:S(2)}) collective-permute-start(f32[4,4,64,2]{3,2,1,0:T(8,128)S(1)} %get-tuple-element.5), channel_id=1, source_target_pairs={{1,0},{2,1},{3,2},{4,3},{5,4},{6,5},{7,6},{8,7},{9,8},{10,9},{11,1... | collective-permute-start | bytes 24584 | tf_op jit(solution)/shard_map/ppermute | solution.py:21
  43.0 13.2 %collective-permute-start.2 = (f32[4,3,32,1]{3,2,1,0:T(8,128)S(1)}, f32[4,3,32,1]{3,2,1,0:T(8,128)S(1)}, u32[]{:S(2)}, u32[]{:S(2)}) collective-permute-start(f32[4,3,32,1]{3,2,1,0:T(8,128)S(1)} %get-tuple-element.11), channel_id=1, source_target_pairs={{0,1},{1,2},{2,3},{3,4},{4,5},{5,6},{6,7},{7,8},{8,9},{9,10},{10,1... | collective-permute-start | bytes 4616 | tf_op jit(solution)/shard_map/ppermute | solution.py:20
  44.9 11.3 %collective-permute-start.3 = (f32[4,3,32,1]{3,2,1,0:T(8,128)S(1)}, f32[4,3,32,1]{3,2,1,0:T(8,128)S(1)}, u32[]{:S(2)}, u32[]{:S(2)}) collective-permute-start(f32[4,3,32,1]{3,2,1,0:T(8,128)S(1)} %get-tuple-element.12), channel_id=1, source_target_pairs={{1,0},{2,1},{3,2},{4,3},{5,4},{6,5},{7,6},{8,7},{9,8},{10,9},{11,1... | collective-permute-start | bytes 4616 | tf_op jit(solution)/shard_map/ppermute | solution.py:21
  47.4 25.1 %collective-permute-start.4 = (f32[4,4,32,2]{3,2,1,0:T(8,128)S(1)}, f32[4,4,32,2]{3,2,1,0:T(8,128)}, u32[]{:S(2)}, u32[]{:S(2)}) collective-permute-start(f32[4,4,32,2]{3,2,1,0:T(8,128)S(1)} %get-tuple-element.9), channel_id=1, source_target_pairs={{0,1},{1,2},{2,3},{3,4},{4,5},{5,6},{6,7},{7,8},{8,9},{9,10},{10,1... | collective-permute-start | bytes 12296 | tf_op jit(solution)/shard_map/ppermute | solution.py:20
  53.9 18.6 %collective-permute-start.5 = (f32[4,4,32,2]{3,2,1,0:T(8,128)S(1)}, f32[4,4,32,2]{3,2,1,0:T(8,128)}, u32[]{:S(2)}, u32[]{:S(2)}) collective-permute-start(f32[4,4,32,2]{3,2,1,0:T(8,128)S(1)} %get-tuple-element.10), channel_id=1, source_target_pairs={{1,0},{2,1},{3,2},{4,3},{5,4},{6,5},{7,6},{8,7},{9,8},{10,9},{11,1... | collective-permute-start | bytes 12296 | tf_op jit(solution)/shard_map/ppermute | solution.py:21
  75.9 18.1 %collective-permute-start.6 = (f32[4,3,16,1]{3,2,1,0:T(8,128)S(1)}, f32[4,3,16,1]{3,2,1,0:T(8,128)S(1)}, u32[]{:S(2)}, u32[]{:S(2)}) collective-permute-start(f32[4,3,16,1]{3,2,1,0:T(8,128)S(1)} %get-tuple-element.17), channel_id=1, source_target_pairs={{0,1},{1,2},{2,3},{3,4},{4,5},{5,6},{6,7},{7,8},{8,9},{9,10},{10,1... | collective-permute-start | bytes 2312 | tf_op jit(solution)/shard_map/ppermute | solution.py:20
  82.9 11.1 %collective-permute-start.7 = (f32[4,3,16,1]{3,2,1,0:T(8,128)S(1)}, f32[4,3,16,1]{3,2,1,0:T(8,128)S(1)}, u32[]{:S(2)}, u32[]{:S(2)}) collective-permute-start(f32[4,3,16,1]{3,2,1,0:T(8,128)S(1)} %get-tuple-element.18), channel_id=1, source_target_pairs={{1,0},{2,1},{3,2},{4,3},{5,4},{6,5},{7,6},{8,7},{9,8},{10,9},{11,1... | collective-permute-start | bytes 2312 | tf_op jit(solution)/shard_map/ppermute | solution.py:21
  84.9 11.2 %collective-permute-start.8 = (f32[4,4,16,2]{3,2,1,0:T(8,128)S(1)}, f32[4,4,16,2]{3,2,1,0:T(8,128)S(1)}, u32[]{:S(2)}, u32[]{:S(2)}) collective-permute-start(f32[4,4,16,2]{3,2,1,0:T(8,128)S(1)} %get-tuple-element.15), channel_id=1, source_target_pairs={{0,1},{1,2},{2,3},{3,4},{4,5},{5,6},{6,7},{7,8},{8,9},{9,10},{10,1... | collective-permute-start | bytes 6152 | tf_op jit(solution)/shard_map/ppermute | solution.py:20
  91.8 9.6 %copy-start.3 = (s32[128]{0:T(128)S(1)}, s32[128]{0:T(128)}, u32[]{:S(2)}) copy-start(s32[128]{0:T(128)} %iota_multiply_fusion.5) | copy-start | bytes 1540
  91.8 9.6 %collective-permute-start.9 = (f32[4,4,16,2]{3,2,1,0:T(8,128)S(1)}, f32[4,4,16,2]{3,2,1,0:T(8,128)S(1)}, u32[]{:S(2)}, u32[]{:S(2)}) collective-permute-start(f32[4,4,16,2]{3,2,1,0:T(8,128)S(1)} %get-tuple-element.16), channel_id=1, source_target_pairs={{1,0},{2,1},{3,2},{4,3},{5,4},{6,5},{7,6},{8,7},{9,8},{10,9},{11,1... | collective-permute-start | bytes 6152 | tf_op jit(solution)/shard_map/ppermute | solution.py:21
  96.0 26.2 %copy-start.2 = (s32[64]{0:T(128)S(1)}, s32[64]{0:T(128)}, u32[]{:S(2)}) copy-start(s32[64]{0:T(128)} %iota_multiply_fusion.3) | copy-start | bytes 772
  102.5 12.8 %collective-permute-start.10 = (f32[4,3,8,1]{3,2,1,0:T(8,128)S(1)}, f32[4,3,8,1]{3,2,1,0:T(8,128)S(1)}, u32[]{:S(2)}, u32[]{:S(2)}) collective-permute-start(f32[4,3,8,1]{3,2,1,0:T(8,128)S(1)} %get-tuple-element.27), channel_id=1, source_target_pairs={{0,1},{1,2},{2,3},{3,4},{4,5},{5,6},{6,7},{7,8},{8,9},{9,10},{10,1... | collective-permute-start | bytes 1160 | tf_op jit(solution)/shard_map/ppermute | solution.py:20
  104.4 10.9 %collective-permute-start.11 = (f32[4,3,8,1]{3,2,1,0:T(8,128)S(1)}, f32[4,3,8,1]{3,2,1,0:T(8,128)S(1)}, u32[]{:S(2)}, u32[]{:S(2)}) collective-permute-start(f32[4,3,8,1]{3,2,1,0:T(8,128)S(1)} %get-tuple-element.28), channel_id=1, source_target_pairs={{1,0},{2,1},{3,2},{4,3},{5,4},{6,5},{7,6},{8,7},{9,8},{10,9},{11,1... | collective-permute-start | bytes 1160 | tf_op jit(solution)/shard_map/ppermute | solution.py:21
  106.8 9.2 %collective-permute-start.12 = (f32[4,4,8,2]{3,2,1,0:T(8,128)S(1)}, f32[4,4,8,2]{3,2,1,0:T(8,128)S(1)}, u32[]{:S(2)}, u32[]{:S(2)}) collective-permute-start(f32[4,4,8,2]{3,2,1,0:T(8,128)S(1)} %get-tuple-element.25), channel_id=1, source_target_pairs={{0,1},{1,2},{2,3},{3,4},{4,5},{5,6},{6,7},{7,8},{8,9},{9,10},{10,1... | collective-permute-start | bytes 3080 | tf_op jit(solution)/shard_map/ppermute | solution.py:20
  113.3 8.9 %collective-permute-start.13 = (f32[4,4,8,2]{3,2,1,0:T(8,128)S(1)}, f32[4,4,8,2]{3,2,1,0:T(8,128)S(1)}, u32[]{:S(2)}, u32[]{:S(2)}) collective-permute-start(f32[4,4,8,2]{3,2,1,0:T(8,128)S(1)} %get-tuple-element.26), channel_id=1, source_target_pairs={{1,0},{2,1},{3,2},{4,3},{5,4},{6,5},{7,6},{8,7},{9,8},{10,9},{11,1... | collective-permute-start | bytes 3080 | tf_op jit(solution)/shard_map/ppermute | solution.py:21
  123.0 12.9 %collective-permute-start.16 = (f32[4,4,4,2]{3,2,1,0:T(4,128)S(1)}, f32[4,4,4,2]{3,2,1,0:T(4,128)S(1)}, u32[]{:S(2)}, u32[]{:S(2)}) collective-permute-start(f32[4,4,4,2]{3,2,1,0:T(4,128)S(1)} %get-tuple-element.31), channel_id=1, source_target_pairs={{0,1},{1,2},{2,3},{3,4},{4,5},{5,6},{6,7},{7,8},{8,9},{9,10},{10,1... | collective-permute-start | bytes 1544 | tf_op jit(solution)/shard_map/ppermute | solution.py:20
  125.0 8.0 %collective-permute-start.14 = (f32[4,3,4,1]{3,2,1,0:T(4,128)S(1)}, f32[4,3,4,1]{3,2,1,0:T(4,128)S(1)}, u32[]{:S(2)}, u32[]{:S(2)}) collective-permute-start(f32[4,3,4,1]{3,2,1,0:T(4,128)S(1)} %get-tuple-element.33), channel_id=1, source_target_pairs={{0,1},{1,2},{2,3},{3,4},{4,5},{5,6},{6,7},{7,8},{8,9},{9,10},{10,1... | collective-permute-start | bytes 584 | tf_op jit(solution)/shard_map/ppermute | solution.py:20
  126.9 8.5 %collective-permute-start.15 = (f32[4,3,4,1]{3,2,1,0:T(4,128)S(1)}, f32[4,3,4,1]{3,2,1,0:T(4,128)S(1)}, u32[]{:S(2)}, u32[]{:S(2)}) collective-permute-start(f32[4,3,4,1]{3,2,1,0:T(4,128)S(1)} %get-tuple-element.34), channel_id=1, source_target_pairs={{1,0},{2,1},{3,2},{4,3},{5,4},{6,5},{7,6},{8,7},{9,8},{10,9},{11,1... | collective-permute-start | bytes 584 | tf_op jit(solution)/shard_map/ppermute | solution.py:21
  129.3 8.6 %collective-permute-start.17 = (f32[4,4,4,2]{3,2,1,0:T(4,128)S(1)}, f32[4,4,4,2]{3,2,1,0:T(4,128)S(1)}, u32[]{:S(2)}, u32[]{:S(2)}) collective-permute-start(f32[4,4,4,2]{3,2,1,0:T(4,128)S(1)} %get-tuple-element.32), channel_id=1, source_target_pairs={{1,0},{2,1},{3,2},{4,3},{5,4},{6,5},{7,6},{8,7},{9,8},{10,9},{11,1... | collective-permute-start | bytes 1544 | tf_op jit(solution)/shard_map/ppermute | solution.py:21
  139.9 15.2 %all-to-all-start.5 = ((bf16[4,3,1,32]{3,1,2,0:T(4,128)(2,1)}), bf16[4,3,1,32]{3,1,2,0:T(4,128)(2,1)S(1)}, u32[]{:S(2)}, u32[]{:S(2)}) async-start(bf16[4,3,1,32]{3,1,2,0:T(4,128)(2,1)} %convert_bitcast_fusion.1), calls=%async_computation.5 | async-start | bytes 8192 | tf_op jit(solution)/shard_map/all_to_all | solution.py:123
  144.0 4.3 %collective-permute-start.18 = (f32[4,3,2,1]{3,2,1,0:T(2,128)S(1)}, f32[4,3,2,1]{3,2,1,0:T(2,128)S(1)}, u32[]{:S(2)}, u32[]{:S(2)}) collective-permute-start(f32[4,3,2,1]{3,2,1,0:T(2,128)S(1)} %get-tuple-element.41), channel_id=1, source_target_pairs={{0,1},{1,2},{2,3},{3,4},{4,5},{5,6},{6,7},{7,8},{8,9},{9,10},{10,1... | collective-permute-start | bytes 296 | tf_op jit(solution)/shard_map/ppermute | solution.py:20
  146.1 8.3 %collective-permute-start.19 = (f32[4,3,2,1]{3,2,1,0:T(2,128)S(1)}, f32[4,3,2,1]{3,2,1,0:T(2,128)S(1)}, u32[]{:S(2)}, u32[]{:S(2)}) collective-permute-start(f32[4,3,2,1]{3,2,1,0:T(2,128)S(1)} %get-tuple-element.42), channel_id=1, source_target_pairs={{1,0},{2,1},{3,2},{4,3},{5,4},{6,5},{7,6},{8,7},{9,8},{10,9},{11,1... | collective-permute-start | bytes 296 | tf_op jit(solution)/shard_map/ppermute | solution.py:21
  155.2 11.4 %collective-permute-start.20 = (f32[3,1,32]{2,1,0:T(1,128)S(1)}, f32[3,1,32]{2,1,0:T(1,128)S(1)}, u32[]{:S(2)}, u32[]{:S(2)}) collective-permute-start(f32[3,1,32]{2,1,0:T(1,128)S(1)} %copy.41), channel_id=1, source_target_pairs={{0,64},{64,128},{128,192},{1,65},{65,129},{129,193},{2,66},{66,130... | collective-permute-start | bytes 1160 | tf_op jit(solution)/shard_map/ppermute | solution.py:20
  158.8 7.7 %collective-permute-start.21 = (f32[3,1,32]{2,1,0:T(1,128)S(1)}, f32[3,1,32]{2,1,0:T(1,128)S(1)}, u32[]{:S(2)}, u32[]{:S(2)}) collective-permute-start(f32[3,1,32]{2,1,0:T(1,128)S(1)} %copy.41), channel_id=1, source_target_pairs={{64,0},{128,64},{192,128},{65,1},{129,65},{193,129},{66,2},{130,66... | collective-permute-start | bytes 1160 | tf_op jit(solution)/shard_map/ppermute | solution.py:21
  161.7 16.3 %all-to-all-start.4 = ((bf16[4,2,192]{2,1,0:T(2,128)(2,1)}), bf16[4,2,192]{2,1,0:T(2,128)(2,1)S(1)}, u32[]{:S(2)}, u32[]{:S(2)}) async-start(bf16[4,2,192]{2,1,0:T(2,128)(2,1)} %reshape.812), calls=%async_computation.4 | async-start | bytes 8192 | tf_op jit(solution)/shard_map/all_to_all | solution.py:123
  166.6 4.7 %collective-permute-start.22 = (f32[3,3,1]{2,1,0:T(4,128)S(1)}, f32[3,3,1]{2,1,0:T(4,128)S(1)}, u32[]{:S(2)}, u32[]{:S(2)}) collective-permute-start(f32[3,3,1]{2,1,0:T(4,128)S(1)} %get-tuple-element.51), channel_id=1, source_target_pairs={{0,1},{1,2},{2,3},{3,4},{4,5},{5,6},{6,7},{7,8},{8,9},{9,10},{10,1... | collective-permute-start | bytes 116 | tf_op jit(solution)/shard_map/ppermute | solution.py:20
  169.4 8.3 %collective-permute-start.23 = (f32[3,3,1]{2,1,0:T(4,128)S(1)}, f32[3,3,1]{2,1,0:T(4,128)S(1)}, u32[]{:S(2)}, u32[]{:S(2)}) collective-permute-start(f32[3,3,1]{2,1,0:T(4,128)S(1)} %get-tuple-element.52), channel_id=1, source_target_pairs={{1,0},{2,1},{3,2},{4,3},{5,4},{6,5},{7,6},{8,7},{9,8},{10,9},{11,1... | collective-permute-start | bytes 116 | tf_op jit(solution)/shard_map/ppermute | solution.py:21
  178.3 11.3 %collective-permute-start.24 = (f32[3,1,64]{2,1,0:T(1,128)S(1)}, f32[3,1,64]{2,1,0:T(1,128)S(1)}, u32[]{:S(2)}, u32[]{:S(2)}) collective-permute-start(f32[3,1,64]{2,1,0:T(1,128)S(1)} %get-tuple-element.55), channel_id=1, source_target_pairs={{0,64},{64,128},{128,192},{1,65},{65,129},{129,193},{2,66},{66,130... | collective-permute-start | bytes 2312 | tf_op jit(solution)/shard_map/ppermute | solution.py:20
  181.9 7.7 %collective-permute-start.25 = (f32[3,1,64]{2,1,0:T(1,128)S(1)}, f32[3,1,64]{2,1,0:T(1,128)S(1)}, u32[]{:S(2)}, u32[]{:S(2)}) collective-permute-start(f32[3,1,64]{2,1,0:T(1,128)S(1)} %get-tuple-element.56), channel_id=1, source_target_pairs={{64,0},{128,64},{192,128},{65,1},{129,65},{193,129},{66,2},{130,66... | collective-permute-start | bytes 2312 | tf_op jit(solution)/shard_map/ppermute | solution.py:21
  184.7 16.3 %all-to-all-start.3 = ((bf16[4,3,4,128]{3,2,1,0:T(4,128)(2,1)}), bf16[4,3,4,128]{3,2,1,0:T(4,128)(2,1)S(1)}, u32[]{:S(2)}, u32[]{:S(2)}) async-start(bf16[4,3,4,128]{3,2,1,0:T(4,128)(2,1)} %convert_element_type.141), calls=%async_computation.3 | async-start | bytes 24576 | tf_op jit(solution)/shard_map/all_to_all | solution.py:123
  189.7 4.7 %collective-permute-start.26 = (f32[3,4,1]{2,1,0:T(4,128)S(1)}, f32[3,4,1]{2,1,0:T(4,128)S(1)}, u32[]{:S(2)}, u32[]{:S(2)}) collective-permute-start(f32[3,4,1]{2,1,0:T(4,128)S(1)} %get-tuple-element.49), channel_id=1, source_target_pairs={{0,1},{1,2},{2,3},{3,4},{4,5},{5,6},{6,7},{7,8},{8,9},{9,10},{10,1... | collective-permute-start | bytes 152 | tf_op jit(solution)/shard_map/ppermute | solution.py:20
  192.5 8.3 %collective-permute-start.27 = (f32[3,4,1]{2,1,0:T(4,128)S(1)}, f32[3,4,1]{2,1,0:T(4,128)S(1)}, u32[]{:S(2)}, u32[]{:S(2)}) collective-permute-start(f32[3,4,1]{2,1,0:T(4,128)S(1)} %get-tuple-element.50), channel_id=1, source_target_pairs={{1,0},{2,1},{3,2},{4,3},{5,4},{6,5},{7,6},{8,7},{9,8},{10,9},{11,1... | collective-permute-start | bytes 152 | tf_op jit(solution)/shard_map/ppermute | solution.py:21
  201.2 11.4 %collective-permute-start.28 = (f32[3,1,128]{2,1,0:T(1,128)S(1)}, f32[3,1,128]{2,1,0:T(1,128)S(1)}, u32[]{:S(2)}, u32[]{:S(2)}) collective-permute-start(f32[3,1,128]{2,1,0:T(1,128)S(1)} %get-tuple-element.47), channel_id=1, source_target_pairs={{0,64},{64,128},{128,192},{1,65},{65,129},{129,193},{2,66},{66,130... | collective-permute-start | bytes 4616 | tf_op jit(solution)/shard_map/ppermute | solution.py:20
  204.9 7.7 %collective-permute-start.29 = (f32[3,1,128]{2,1,0:T(1,128)S(1)}, f32[3,1,128]{2,1,0:T(1,128)S(1)}, u32[]{:S(2)}, u32[]{:S(2)}) collective-permute-start(f32[3,1,128]{2,1,0:T(1,128)S(1)} %get-tuple-element.48), channel_id=1, source_target_pairs={{64,0},{128,64},{192,128},{65,1},{129,65},{193,129},{66,2},{130,66... | collective-permute-start | bytes 4616 | tf_op jit(solution)/shard_map/ppermute | solution.py:21
  207.7 16.4 %all-to-all-start.2 = ((bf16[4,3,8,256]{3,2,1,0:T(8,128)(2,1)}), bf16[4,3,8,256]{3,2,1,0:T(8,128)(2,1)S(1)}, u32[]{:S(2)}, u32[]{:S(2)}) async-start(bf16[4,3,8,256]{3,2,1,0:T(8,128)(2,1)} %convert_element_type.136), calls=%async_computation.2 | async-start | bytes 98304 | tf_op jit(solution)/shard_map/all_to_all | solution.py:123
  212.7 4.7 %collective-permute-start.30 = (f32[3,6,1]{2,1,0:T(8,128)S(1)}, f32[3,6,1]{2,1,0:T(8,128)S(1)}, u32[]{:S(2)}, u32[]{:S(2)}) collective-permute-start(f32[3,6,1]{2,1,0:T(8,128)S(1)} %get-tuple-element.43), channel_id=1, source_target_pairs={{0,1},{1,2},{2,3},{3,4},{4,5},{5,6},{6,7},{7,8},{8,9},{9,10},{10,1... | collective-permute-start | bytes 224 | tf_op jit(solution)/shard_map/ppermute | solution.py:20
  215.5 8.3 %collective-permute-start.31 = (f32[3,6,1]{2,1,0:T(8,128)S(1)}, f32[3,6,1]{2,1,0:T(8,128)S(1)}, u32[]{:S(2)}, u32[]{:S(2)}) collective-permute-start(f32[3,6,1]{2,1,0:T(8,128)S(1)} %get-tuple-element.44), channel_id=1, source_target_pairs={{1,0},{2,1},{3,2},{4,3},{5,4},{6,5},{7,6},{8,7},{9,8},{10,9},{11,1... | collective-permute-start | bytes 224 | tf_op jit(solution)/shard_map/ppermute | solution.py:21
  224.4 7.0 %collective-permute-start.32 = (f32[3,1,256]{2,1,0:T(1,128)S(1)}, f32[3,1,256]{2,1,0:T(1,128)S(1)}, u32[]{:S(2)}, u32[]{:S(2)}) collective-permute-start(f32[3,1,256]{2,1,0:T(1,128)S(1)} %get-tuple-element.35), channel_id=1, source_target_pairs={{0,64},{64,128},{128,192},{1,65},{65,129},{129,193},{2,66},{66,130... | collective-permute-start | bytes 9224 | tf_op jit(solution)/shard_map/ppermute | solution.py:20
  228.0 4.3 %collective-permute-start.33 = (f32[3,1,256]{2,1,0:T(1,128)S(1)}, f32[3,1,256]{2,1,0:T(1,128)S(1)}, u32[]{:S(2)}, u32[]{:S(2)}) collective-permute-start(f32[3,1,256]{2,1,0:T(1,128)S(1)} %get-tuple-element.36), channel_id=1, source_target_pairs={{64,0},{128,64},{192,128},{65,1},{129,65},{193,129},{66,2},{130,66... | collective-permute-start | bytes 9224 | tf_op jit(solution)/shard_map/ppermute | solution.py:21
  232.5 9.0 %collective-permute-start.34 = (f32[3,10,1]{2,1,0:T(8,128)S(1)}, f32[3,10,1]{2,1,0:T(8,128)S(1)}, u32[]{:S(2)}, u32[]{:S(2)}) collective-permute-start(f32[3,10,1]{2,1,0:T(8,128)S(1)} %get-tuple-element.29), channel_id=1, source_target_pairs={{0,1},{1,2},{2,3},{3,4},{4,5},{5,6},{6,7},{7,8},{8,9},{9,10},{10,1... | collective-permute-start | bytes 368 | tf_op jit(solution)/shard_map/ppermute | solution.py:20
  235.8 8.5 %collective-permute-start.35 = (f32[3,10,1]{2,1,0:T(8,128)S(1)}, f32[3,10,1]{2,1,0:T(8,128)S(1)}, u32[]{:S(2)}, u32[]{:S(2)}) collective-permute-start(f32[3,10,1]{2,1,0:T(8,128)S(1)} %get-tuple-element.30), channel_id=1, source_target_pairs={{1,0},{2,1},{3,2},{4,3},{5,4},{6,5},{7,6},{8,7},{9,8},{10,9},{11,1... | collective-permute-start | bytes 368 | tf_op jit(solution)/shard_map/ppermute | solution.py:21
  237.8 10.2 %all-to-all-start.1 = ((bf16[4,3,16,512]{3,2,1,0:T(8,128)(2,1)}), bf16[4,3,16,512]{3,2,1,0:T(8,128)(2,1)S(1)}, u32[]{:S(2)}, u32[]{:S(2)}) async-start(bf16[4,3,16,512]{3,2,1,0:T(8,128)(2,1)} %convert_element_type.131), calls=%async_computation.1 | async-start | bytes 393216 | tf_op jit(solution)/shard_map/all_to_all | solution.py:123
  247.9 31.8 %all-to-all-start = ((bf16[4,3,32,1024]{3,2,1,0:T(8,128)(2,1)}), bf16[4,3,32,1024]{3,2,1,0:T(8,128)(2,1)S(1)}, u32[]{:S(2)}, u32[]{:S(2)}) async-start(bf16[4,3,32,1024]{3,2,1,0:T(8,128)(2,1)} %convert_element_type.126), calls=%async_computation | async-start | bytes 1572864 | tf_op jit(solution)/shard_map/all_to_all | solution.py:123
  251.8 8.3 %collective-permute-start.36 = (f32[3,1,512]{2,1,0:T(1,128)S(1)}, f32[3,1,512]{2,1,0:T(1,128)S(1)}, u32[]{:S(2)}, u32[]{:S(2)}) collective-permute-start(f32[3,1,512]{2,1,0:T(1,128)S(1)} %get-tuple-element.21), channel_id=1, source_target_pairs={{0,64},{64,128},{128,192},{1,65},{65,129},{129,193},{2,66},{66,130... | collective-permute-start | bytes 18440 | tf_op jit(solution)/shard_map/ppermute | solution.py:20
  255.1 6.9 %collective-permute-start.37 = (f32[3,1,512]{2,1,0:T(1,128)S(1)}, f32[3,1,512]{2,1,0:T(1,128)S(1)}, u32[]{:S(2)}, u32[]{:S(2)}) collective-permute-start(f32[3,1,512]{2,1,0:T(1,128)S(1)} %get-tuple-element.22), channel_id=1, source_target_pairs={{64,0},{128,64},{192,128},{65,1},{129,65},{193,129},{66,2},{130,66... | collective-permute-start | bytes 18440 | tf_op jit(solution)/shard_map/ppermute | solution.py:21
  262.1 8.5 %collective-permute-start.38 = (f32[3,18,1]{2,1,0:T(8,128)S(1)}, f32[3,18,1]{2,1,0:T(8,128)S(1)}, u32[]{:S(2)}, u32[]{:S(2)}) collective-permute-start(f32[3,18,1]{2,1,0:T(8,128)S(1)} %get-tuple-element.19), channel_id=1, source_target_pairs={{0,1},{1,2},{2,3},{3,4},{4,5},{5,6},{6,7},{7,8},{8,9},{9,10},{10,1... | collective-permute-start | bytes 656 | tf_op jit(solution)/shard_map/ppermute | solution.py:20
  268.4 8.6 %collective-permute-start.39 = (f32[3,18,1]{2,1,0:T(8,128)S(1)}, f32[3,18,1]{2,1,0:T(8,128)S(1)}, u32[]{:S(2)}, u32[]{:S(2)}) collective-permute-start(f32[3,18,1]{2,1,0:T(8,128)S(1)} %get-tuple-element.20), channel_id=1, source_target_pairs={{1,0},{2,1},{3,2},{4,3},{5,4},{6,5},{7,6},{8,7},{9,8},{10,9},{11,1... | collective-permute-start | bytes 656 | tf_op jit(solution)/shard_map/ppermute | solution.py:21
  (2 other events, 13.0 us)
where the time goes:
time: 283 us; the launch traced here: 281 us
  starting transfers between devices  143 us (51%)
  waiting for transfers between devices  67.5 us (24%)
  matrix products  37.9 us (13%)
  other arithmetic  21.8 us (8%)
  local copies, waits for them, and re-layouts  9.76 us (3%)
    ppermute x20, starting transfers between devices, extended(): before = lax.ppermute(last, axis, up)  77.6 us
    ppermute x20, waiting for transfers between devices, extended(): after = lax.ppermute(initial, axis, down)  60.9 us
    ppermute x20, starting transfers between devices, extended(): after = lax.ppermute(initial, axis, down)  39.5 us
    dot_general x15, matrix products, apply_columns(): return jnp.matmul(field, matrix, precision=highest)  28.3 us
    all_to_all x6, starting transfers between devices, per_device(): lax.all_to_all(for_sending(parts), 'strip', split_axis=0, concat_axis=0,...  25.8 us
    dot_general x15, matrix products, apply_rows(): return jnp.einsum('...rw,rs->...sw', field, matrix, precision=highest)  9.54 us
    scatter-add x6, other arithmetic, gather_blocks(): return buffer.at[targets].add(blocks).astype(jnp.bfloat16)  9.43 us
    concatenate x1, local copies, waits for them, and re-layouts, extended(): x = jnp.concatenate([before, x, after], axis=dim)  6.38 us
  transfers between devices with their start and end apart: 46, of which 15 were waited for; matrix products, arithmetic and copies ran while one was open for 13% of the time, Pallas kernels for 0%

commit v1 on v0

v1 whole, which is shorter than its diff:
```python
import functools

import jax
import jax.numpy as jnp
import ml_dtypes
import numpy as np
from jax import lax
from jax.experimental import pallas as pl
from jax.experimental.pallas import tpu as pltpu
from jax.sharding import PartitionSpec as P

BF = jnp.bfloat16
F32 = jnp.float32
MESH = pl.DeviceIdType.MESH
TAPS = (0.0625, 0.25, 0.375, 0.25, 0.0625)
N = 1024
HALO = 128
WIDE = {0: 1280, 1: 640, 2: 320, 3: 160, 4: 80, 5: 40}
PAD = {1: 640, 2: 384, 3: 256, 4: 128, 5: 128}
ROWS = {0: 64, 1: 32, 2: 16, 3: 8, 4: 4, 5: 2}
SLOT = {2: (0, 64), 3: (64, 32), 4: (96, 16), 5: (112, 16)}


def reduce_rows(tall):
    m = np.zeros((tall // 2, tall))
    for i in range(tall // 2):
        for t in range(5):
            r = 2 * i + t - 2
            if 0 <= r < tall:
                m[i, r] = TAPS[t]
    return m


def expand_rows(tall):
    m = np.zeros((2 * tall, tall))
    for i in range(tall):
        for r, w in ((i - 1, 0.125), (i, 0.75), (i + 1, 0.125)):
            if 0 <= r < tall:
                m[2 * i, r] = w
        for r in (i, i + 1):
            if r < tall:
                m[2 * i + 1, r] = 0.5
    return m


def blocks(m, count):
    return np.kron(np.eye(count), m)


def bf(x):
    return np.asarray(x, np.float32).astype(ml_dtypes.bfloat16)


def split(x):
    hi = bf(x)
    return hi, bf(np.asarray(x, np.float64) - hi.astype(np.float64))


def valid(level, edge):
    e = np.arange(WIDE[level])
    h = HALO >> level
    n = N >> level
    keep = np.ones(WIDE[level])
    if edge == 0:
        keep[e < h] = 0
    if edge == 2:
        keep[e >= h + n] = 0
    return keep


def reduce_cols(level, edge):
    m = reduce_rows(WIDE[level]).T
    return m * valid(level + 1, edge)[None, :]


def constants():
    c = {}
    c["v1"] = bf(blocks(reduce_rows(64), 4))
    w = np.zeros((512, 128))
    for col in range(128):
        for t in range(5):
            w[128 + 2 * col + t - 2, col] = TAPS[t]
    c["wred"] = bf(w)
    v = {1: np.eye(32)}
    for k in (2, 3, 4, 5):
        v[k] = reduce_rows(ROWS[k - 1]) @ v[k - 1]
    v25 = np.zeros((128, 128))
    for k in (2, 3, 4, 5):
        start, _ = SLOT[k]
        v25[start : start + 4 * ROWS[k]] = blocks(v[k], 4)
    c["v25"] = bf(v25)
    h35 = np.zeros((3, 384, 384))
    for edge in range(3):
        m3 = reduce_cols(2, edge)
        m4 = m3 @ reduce_cols(3, edge)
        m5 = m4 @ reduce_cols(4, edge)
        h35[edge, :320, 0:160] = m3
        h35[edge, :320, 256:336] = m4
        h35[edge, :320, 336:376] = m5
    c["h35"] = bf(h35)
    c["er1"] = bf(blocks(expand_rows(16), 12))
    c["er2"] = bf(blocks(expand_rows(8), 12))
    c["er3"] = bf(blocks(expand_rows(4), 12))
    er4 = np.zeros((48, 48))
    for ch in range(3):
        er4[16 * ch : 16 * ch + 16, 16 * ch : 16 * ch + 8] = blocks(expand_rows(2), 4)
    c["er4"] = bf(er4)
    for k in (1, 2, 3, 4):
        m = np.zeros((PAD[k + 1], PAD[k]))
        at = 80 if k == 4 else 0
        m[at : at + WIDE[k + 1], : WIDE[k]] = expand_rows(WIDE[k + 1]).T
        c[f"ec{k}"] = bf(m)
    e0 = np.zeros((256, 256))
    for col in range(256):
        i = 64 + col // 2
        if col % 2 == 0:
            e0[i - 1, col], e0[i, col], e0[i + 1, col] = 0.125, 0.75, 0.125
        else:
            e0[i, col], e0[i + 1, col] = 0.5, 0.5
    c["e0"] = bf(e0)
    er0 = -blocks(expand_rows(32), 4)
    c["d0"] = bf(np.concatenate([np.eye(256), er0, er0], axis=1))
    hi = np.zeros((3, 64, 640))
    lo = np.zeros((3, 64, 640))
    for first in range(3):
        up = np.eye(64)
        for k in (1, 2, 3, 4, 5):
            h = 32 >> k
            if k > 1:
                up = up @ expand_rows(4 * h)
            place = np.zeros((4 * h, 2 * h))
            place[first * h : first * h + 2 * h] = np.eye(2 * h)
            m = np.tile(up @ place, (1, 4))
            a, b = split(m)
            s = 128 * (k - 1)
            hi[first, :, s : s + m.shape[1]] = a.astype(np.float64)
            lo[first, :, s : s + m.shape[1]] = b.astype(np.float64)
    c["lb"] = bf(hi)
    c["lb5"] = bf(lo[:, :, 384:])
    assert not lo[:, :, :384].any()
    pm = np.full((8, 640), -1.0)
    for k in (1, 2, 3, 4, 5):
        for p in range(4):
            s = 128 * (k - 1) + p * ROWS[k]
            pm[:, s : s + ROWS[k]] = p
    c["pm"] = pm.astype(np.float32)
    return c


NAMES = ("v1", "wred", "v25", "h35", "er1", "er2", "er3", "er4", "ec1", "ec2", "ec3", "ec4", "e0", "d0", "lb", "lb5", "pm")


def dot(a, b):
    return jnp.dot(a, b, preferred_element_type=F32)


def halves(x):
    hi = x.astype(BF)
    return hi, (x - hi.astype(F32)).astype(BF)


def kernel(n_strip, n_lvl, offsets, photos, seams, v1, wred, v25, h35, er1, er2, er3, er4, ec1, ec2, ec3, ec4, e0, d0, lb, lb5, pm,
           out, s0, s1, tm, g1, ys, y2, c1h, c1l, send2, sendd, keep, relay, r1, r2, r3,
           halo_send, halo_recv, m1_send, m1_recv, m2_send, m2_recv, m3_send, m3_recv):
    x = lax.axis_index("strip")
    me = lax.axis_index("lvl")
    right, left = lax.rem(me + 1, n_lvl), lax.rem(me + n_lvl - 1, n_lvl)
    up, down = lax.rem(x + 1, n_strip), lax.rem(x + n_strip - 1, n_strip)
    barrier = pltpu.get_barrier_semaphore()
    for target in ({"lvl": left}, {"lvl": right}, {"strip": up}, {"strip": down}):
        pl.semaphore_signal(barrier, inc=1, device_id=target, device_id_type=MESH)

    r_i = lax.broadcasted_iota(jnp.int32, (64, 64), 0)
    c_i = lax.broadcasted_iota(jnp.int32, (64, 64), 1)
    eye = r_i == c_i
    for p in range(4):
        for e, dst in ((0, s0), (1, s1)):
            line = seams[p, e : e + 1, :].astype(F32)
            col = jnp.sum(jnp.where(eye, line, 0.0), axis=1, keepdims=True)
            dst[64 * p : 64 * p + 64, :] = jnp.broadcast_to(col, (64, 128))

    first_col = (me * N).astype(F32)

    def mask_tile(start):
        col = lax.broadcasted_iota(jnp.int32, (256, 128), 1).astype(F32) + (first_col + (start - HALO))
        return (col >= s0[...]) & (col < s1[...])

    def rows_of(ch, start, width):
        return photos[:, ch, :, start : start + width].reshape(256, width)

    lead = v1[...]
    for start in (0, N - 128):
        for ch in range(3):
            tm[ch, :, HALO + start : HALO + start + 128] = dot(lead, rows_of(ch, start, 128)).astype(BF)
    pl.semaphore_wait(barrier, 4)
    halo = []
    for i, (src, dst, target) in enumerate(((HALO, HALO + N, left), (N, 0, right))):
        copy = pltpu.make_async_remote_copy(
            src_ref=tm.at[0:3, :, src : src + 128],
            dst_ref=tm.at[0:3, :, dst : dst + 128],
            send_sem=halo_send.at[i],
            recv_sem=halo_recv.at[i],
            device_id={"lvl": target},
            device_id_type=MESH,
        )
        copy.start()
        halo.append(copy)
    for ch in range(3):
        tm[ch, :, 256 : N] = dot(lead, rows_of(ch, 128, N - 256)).astype(BF)
    for start in range(0, N + 256, 128):
        m = jnp.where(mask_tile(start), 1.0, 0.0).astype(BF)
        tm[3, :, start : start + 128] = dot(lead, m).astype(BF)

    def g1_tile(j):
        a, b = max(0, 2 * j - 1), min(10, 2 * j + 3)
        w = wred[128 * (a - 2 * j + 1) : 128 * (b - 2 * j + 1), :]
        val = dot(tm[:, :, 128 * a : 128 * b].reshape(512, 128 * (b - a)), w)
        if j in (0, 4):
            col = lax.broadcasted_iota(jnp.int32, (1, 128), 1) + (128 * j - 64) + me * (N // 2)
            val = jnp.where((col >= 0) & (col < n_lvl * (N // 2)), val, 0.0)
        g1[:, 128 * j : 128 * j + 128] = val.astype(BF)

    for j in (1, 2, 3):
        g1_tile(j)
    for copy in halo:
        copy.wait()

    @pl.when(me == 0)
    def _():
        tm[0:3, :, 0:128] = jnp.zeros((3, 128, 128), BF)

    @pl.when(me == n_lvl - 1)
    def _():
        tm[0:3, :, N + 128 : N + 256] = jnp.zeros((3, 128, 128), BF)

    for j in (0, 4):
        g1_tile(j)

    for ch in range(4):
        ys[128 * ch : 128 * ch + 128, :] = dot(v25[...], g1[128 * ch : 128 * ch + 128, :]).astype(BF)
    col = lax.broadcasted_iota(jnp.int32, (1, 384), 1) - 32 + me * (N // 4)
    inside = (col >= 0) & (col < n_lvl * (N // 4))
    for j, a, b in ((0, 0, 3), (1, 1, 5), (2, 3, 5)):
        w = wred[128 * (a - 2 * j + 1) : 128 * (b - 2 * j + 1), :]
        val = dot(ys[:, 128 * a : 128 * b], w)
        y2[:, 128 * j : 128 * j + 128] = jnp.where(inside[:, 128 * j : 128 * j + 128], val, 0.0).astype(BF)
    edge = jnp.where(me == 0, 0, jnp.where(me == n_lvl - 1, 2, 1))
    y = y2[...].reshape(4, 128, 384)
    g2 = y[:, 0:64].reshape(256, 384)
    y35 = dot(y[:, 64:128].reshape(256, 384), h35[edge]).astype(BF).reshape(4, 64, 384)
    g3 = y35[:, 0:32, 0:256].reshape(128, 256)
    g4 = y35[:, 32:48, 256:384].reshape(64, 128)
    g5 = y35[:, 48:64, 256:384].reshape(64, 128)
    gs = {1: g1[...], 2: g2, 3: g3, 4: g4, 5: g5}

    weighted = {}
    for k, er, ec, color in ((4, er4, ec4, 48), (3, er3, ec3, 48), (2, er2, ec2, 96), (1, er1, ec1, 192)):
        tall = 4 * ROWS[k]
        u_hi, u_lo = halves(dot(er[...], gs[k + 1][0:color]))
        expanded = dot(jnp.concatenate([u_hi, u_lo], axis=0), ec[...])
        half = 3 * tall
        g = gs[k].astype(F32)
        detail = g[0:half] - (expanded[0:half] + expanded[half:])
        m = g[half:]
        weighted[k] = [(m * detail[ch * tall : ch * tall + tall]).astype(BF) for ch in range(3)]
    g = g5.astype(F32)
    weighted[5] = [(g[48:64] * g[16 * ch : 16 * ch + 16]).astype(BF) for ch in range(3)]

    places = [offsets[p].astype(F32) for p in range(4)]

    def by_photo(which):
        got = jnp.zeros(which.shape, F32)
        for p in range(4):
            got = jnp.where(which == float(p), places[p], got)
        return got

    spot = by_photo(pm[0:1, :])
    table = sum(jnp.where(spot == float(o), lb[o].astype(F32), 0.0) for o in range(3)).astype(BF)
    fine = sum(jnp.where(spot[:, 384:] == float(o), lb5[o].astype(F32), 0.0) for o in range(3)).astype(BF)
    placed = {}
    for k in (5, 4, 3, 2, 1):
        s = 128 * (k - 1)
        size = {1: 128, 2: 64, 3: 32, 4: 16, 5: 16}[k]
        lhs = table[:, s : s + size]
        if k >= 4:
            lhs = jnp.concatenate([lhs, fine[:, s - 384 : s - 384 + size]], axis=0)
        parts = []
        for ch in range(3):
            got = dot(lhs, weighted[k][ch])
            parts.append(got[0:64] + got[64:128] if k >= 4 else got)
        placed[k] = jnp.concatenate(parts, axis=0)

    total = placed[5]
    for k, ec in ((4, ec4), (3, ec3), (2, ec2), (1, ec1)):
        hi, lo = halves(total)
        got = dot(jnp.concatenate([hi, lo], axis=0), ec[...])
        col = lax.broadcasted_iota(jnp.int32, (1, PAD[k]), 1) - (HALO >> k) + me * (N >> k)
        ok = (col >= 0) & (col < n_lvl * (N >> k))
        total = placed[k] + jnp.where(ok, got[0:192] + got[192:384], 0.0)
    hi, lo = halves(total)
    c1h[...] = hi
    c1l[...] = lo

    def strip_rows(width):
        q = lax.broadcasted_iota(jnp.int32, (128, width), 0)
        return ((q >> 5) + x) % 4 * 32 + (q & 31)

    lane = lax.broadcasted_iota(jnp.int32, (128, 256), 1)
    where = by_photo((lane >> 6).astype(F32)).astype(jnp.int32) * 32 + (lane & 63)
    put = jnp.where(strip_rows(256) == where, 1.0, 0.0).astype(BF)
    row = strip_rows(128)
    d = (lax.broadcasted_iota(jnp.int32, (128, 128), 1) & 63) - (row >> 1)
    even = jnp.where(d == 0, 0.75, jnp.where((d == 1) | (d == -1), 0.125, 0.0))
    odd = jnp.where((d == 0) | (d == 1), 0.5, 0.0)
    last = jnp.concatenate([put, jnp.where((row & 1) == 0, even, odd).astype(BF)], axis=1)

    def remote(src, dst, send, recv, target):
        copy = pltpu.make_async_remote_copy(
            src_ref=src, dst_ref=dst, send_sem=send, recv_sem=recv, device_id={"strip": target}, device_id_type=MESH
        )
        copy.start()
        return copy

    order = (0, 2, 1, 3)
    first, direct, second = {}, {}, {}

    def pass_on(t):
        first[t].wait_recv()
        relay[t] = (keep[t] + r1[t].astype(F32)).astype(BF)
        second[t] = remote(relay.at[t], r2.at[t], m2_send.at[t], m2_recv.at[t], up if t < 2 else down)

    for i, t in enumerate(order):
        cols = slice(128 * t, 128 * t + 256)
        lhs = jnp.concatenate([g1[0:384, cols], c1h[:, cols], c1l[:, cols]], axis=0)
        wide = dot(lhs, e0[...])
        u_hi, u_lo = halves(wide[0:384])
        b_hi, b_lo = halves(wide[384:576] + wide[576:768])
        inside = jnp.concatenate([mask_tile(HALO + 256 * t), mask_tile(HALO + 256 * t + 128)], axis=1)
        for ch in range(3):
            r = slice(128 * ch, 128 * ch + 128)
            rhs = jnp.concatenate([rows_of(ch, 256 * t, 256), u_hi[r], u_lo[r]], axis=0)
            band = jnp.where(inside, dot(d0[...], rhs), 0.0).astype(BF)
            r = slice(64 * ch, 64 * ch + 64)
            got = dot(last, jnp.concatenate([band, b_hi[r], b_lo[r]], axis=0))
            out[ch, :, 256 * t : 256 * t + 256] = got[0:32]
            rr = slice(32 * ch, 32 * ch + 32)
            send2[t, rr, :] = got[64:96].astype(BF)
            via, away = (got[32:64], got[96:128]) if t < 2 else (got[96:128], got[32:64])
            keep[t, rr, :] = via
            sendd[t, rr, :] = away.astype(BF)
        forward, back = (up, down) if t < 2 else (down, up)
        first[t] = remote(send2.at[t], r1.at[t], m1_send.at[t], m1_recv.at[t], forward)
        direct[t] = remote(sendd.at[t], r3.at[t], m3_send.at[t], m3_recv.at[t], back)
        if i > 0:
            pass_on(order[i - 1])
    pass_on(order[-1])
    for t in order:
        direct[t].wait_recv()
        second[t].wait_recv()
        got = r2[t].astype(F32) + r3[t].astype(F32)
        for ch in range(3):
            c = slice(256 * t, 256 * t + 256)
            out[ch, :, c] = out[ch, :, c] + got[32 * ch : 32 * ch + 32]
    for t in order:
        first[t].wait_send()
        direct[t].wait_send()
        second[t].wait_send()


def solution(mesh):
    n_strip, n_lvl = mesh.shape["strip"], mesh.shape["lvl"]
    table = constants()

    def per_device(photos, seams, offsets):
        vm = pl.BlockSpec(memory_space=pltpu.VMEM)
        dma = pltpu.SemaphoreType.DMA
        tile = (4, 96, 256)
        return pl.pallas_call(
            functools.partial(kernel, n_strip, n_lvl),
            out_shape=jax.ShapeDtypeStruct((3, 32, N), F32),
            in_specs=[pl.BlockSpec(memory_space=pltpu.SMEM)] + [vm] * (2 + len(NAMES)),
            out_specs=vm,
            scratch_shapes=[
                pltpu.VMEM((256, 128), F32),
                pltpu.VMEM((256, 128), F32),
                pltpu.VMEM((4, 128, 1280), BF),
                pltpu.VMEM((512, 640), BF),
                pltpu.VMEM((512, 640), BF),
                pltpu.VMEM((512, 384), BF),
                pltpu.VMEM((192, 640), BF),
                pltpu.VMEM((192, 640), BF),
                pltpu.VMEM(tile, BF),
                pltpu.VMEM(tile, BF),
                pltpu.VMEM(tile, F32),
                pltpu.VMEM(tile, BF),
                pltpu.VMEM(tile, BF),
                pltpu.VMEM(tile, BF),
                pltpu.VMEM(tile, BF),
                dma((2,)), dma((2,)), dma((4,)), dma((4,)), dma((4,)), dma((4,)), dma((4,)), dma((4,)),
            ],
            compiler_params=pltpu.CompilerParams(collective_id=0, has_side_effects=True, vmem_limit_bytes=50 << 20),
        )(offsets, photos, seams, *[jnp.asarray(table[name]) for name in NAMES])

    placed = (P("strip", None, None, "lvl"), P("strip", None, None), P("strip"))
    return jax.shard_map(
        per_device, mesh=mesh, in_specs=placed, out_specs=P(None, "strip", "lvl"), check_vma=False
    )
```

time: 283 us -> 48.6 us (0.17)
  the two profiles are of different devices: /device:TPU:121 before, /device:TPU:2 now
where the time goes in v1:
time: 48.6 us; the launch traced here: 47.8 us
  Pallas kernels  30.8 us (63%)
  local copies, waits for them, and re-layouts  16.9 us (35%)
    pallas_call x1, Pallas kernels, per_device(): pl.pallas_call(functools.partial(kernel, n_strip, n_lvl), out_shape=jax.S...  30.8 us
    unnamed x39, local copies, waits for them, and re-layouts  16.9 us

profile of v1, /device:TPU:2, one launch (start us, length us, event | category | flops | bytes accessed | tf_op | source)
XLA Modules:
  0.0 47.8 jit_solution(10518577768671239822)
XLA Ops:
  0.0 0.0 copy-start
  0.0 1.2 %copy-done = bf16[3,384,384]{2,1,0:T(8,128)(2,1)S(1)} copy-done((bf16[3,384,384]{2,1,0:T(8,128)(2,1)S(1)}, bf16[3,384,384]{2,1,0:T(8,128)(2,1)}, u32[]{:S(2)}) %copy-start) | copy-done | bytes 884760
  1.2 0.0 copy-start.1
  1.2 1.0 %copy-done.1 = bf16[384,640]{1,0:T(8,128)(2,1)S(1)} copy-done((bf16[384,640]{1,0:T(8,128)(2,1)S(1)}, bf16[384,640]{1,0:T(8,128)(2,1)}, u32[]{:S(2)}) %copy-start.1) | copy-done | bytes 491544
  2.2 0.0 copy-start.2
  2.2 0.9 %copy-done.2 = bf16[256,512]{1,0:T(8,128)(2,1)S(1)} copy-done((bf16[256,512]{1,0:T(8,128)(2,1)S(1)}, bf16[256,512]{1,0:T(8,128)(2,1)}, u32[]{:S(2)}) %copy-start.2) | copy-done | bytes 262168
  3.1 0.0 copy-start.3
  3.2 0.9 %copy-done.3 = bf16[3,64,640]{2,1,0:T(8,128)(2,1)S(1)} copy-done((bf16[3,64,640]{2,1,0:T(8,128)(2,1)S(1)}, bf16[3,64,640]{2,1,0:T(8,128)(2,1)}, u32[]{:S(2)}) %copy-start.3) | copy-done | bytes 245784
  4.1 0.0 copy-start.4
  4.1 0.9 %copy-done.4 = bf16[256,384]{1,0:T(8,128)(2,1)S(1)} copy-done((bf16[256,384]{1,0:T(8,128)(2,1)S(1)}, bf16[256,384]{1,0:T(8,128)(2,1)}, u32[]{:S(2)}) %copy-start.4) | copy-done | bytes 196632
  5.0 0.0 copy-start.5
  5.0 0.9 %copy-done.5 = bf16[384,192]{1,0:T(8,128)(2,1)S(1)} copy-done((bf16[384,192]{1,0:T(8,128)(2,1)S(1)}, bf16[384,192]{1,0:T(8,128)(2,1)}, u32[]{:S(2)}) %copy-start.5) | copy-done | bytes 147480
  5.9 0.0 copy-start.6
  6.0 0.9 %copy-done.6 = bf16[256,256]{1,0:T(8,128)(2,1)S(1)} copy-done((bf16[256,256]{1,0:T(8,128)(2,1)S(1)}, bf16[256,256]{1,0:T(8,128)(2,1)}, u32[]{:S(2)}) %copy-start.6) | copy-done | bytes 131096
  6.9 0.0 copy-start.7
  6.9 0.9 %copy-done.7 = bf16[512,128]{1,0:T(8,128)(2,1)S(1)} copy-done((bf16[512,128]{1,0:T(8,128)(2,1)S(1)}, bf16[512,128]{1,0:T(8,128)(2,1)}, u32[]{:S(2)}) %copy-start.7) | copy-done | bytes 131096
  7.8 0.0 copy-start.8
  7.8 0.9 %copy-done.8 = bf16[3,64,256]{2,1,0:T(8,128)(2,1)S(1)} copy-done((bf16[3,64,256]{2,1,0:T(8,128)(2,1)S(1)}, bf16[3,64,256]{2,1,0:T(8,128)(2,1)}, u32[]{:S(2)}) %copy-start.8) | copy-done | bytes 98328
  8.7 0.0 copy-start.9
  8.7 0.8 %copy-done.9 = bf16[128,256]{1,0:T(8,128)(2,1)S(1)} copy-done((bf16[128,256]{1,0:T(8,128)(2,1)S(1)}, bf16[128,256]{1,0:T(8,128)(2,1)}, u32[]{:S(2)}) %copy-start.9) | copy-done | bytes 65560
  9.5 0.0 copy-start.10
  9.5 0.8 %copy-done.10 = bf16[128,256]{1,0:T(8,128)(2,1)S(1)} copy-done((bf16[128,256]{1,0:T(8,128)(2,1)S(1)}, bf16[128,256]{1,0:T(8,128)(2,1)}, u32[]{:S(2)}) %copy-start.10) | copy-done | bytes 65560
  10.3 0.0 copy-start.11
  10.3 0.8 %copy-done.11 = bf16[192,96]{1,0:T(8,128)(2,1)S(1)} copy-done((bf16[192,96]{1,0:T(8,128)(2,1)S(1)}, bf16[192,96]{1,0:T(8,128)(2,1)}, u32[]{:S(2)}) %copy-start.11) | copy-done | bytes 36888
  11.1 0.0 copy-start.12
  11.1 0.8 %copy-done.12 = bf16[128,128]{1,0:T(8,128)(2,1)S(1)} copy-done((bf16[128,128]{1,0:T(8,128)(2,1)S(1)}, bf16[128,128]{1,0:T(8,128)(2,1)}, u32[]{:S(2)}) %copy-start.12) | copy-done | bytes 32792
  11.9 0.0 copy-start.13
  11.9 0.8 %copy-done.13 = bf16[128,128]{1,0:T(8,128)(2,1)S(1)} copy-done((bf16[128,128]{1,0:T(8,128)(2,1)S(1)}, bf16[128,128]{1,0:T(8,128)(2,1)}, u32[]{:S(2)}) %copy-start.13) | copy-done | bytes 32792
  12.6 0.0 copy-start.14
  12.6 0.7 %copy-done.14 = bf16[96,48]{1,0:T(8,128)(2,1)S(1)} copy-done((bf16[96,48]{1,0:T(8,128)(2,1)S(1)}, bf16[96,48]{1,0:T(8,128)(2,1)}, u32[]{:S(2)}) %copy-start.14) | copy-done | bytes 9240
  13.4 0.0 copy-start.15
  13.4 0.7 %copy-done.15 = f32[8,640]{1,0:T(8,128)S(1)} copy-done((f32[8,640]{1,0:T(8,128)S(1)}, f32[8,640]{1,0:T(8,128)}, u32[]{:S(2)}) %copy-start.15) | copy-done | bytes 20504
  14.1 0.0 copy-start.16
  14.1 0.7 %copy-done.16 = bf16[48,48]{1,0:T(8,128)(2,1)S(1)} copy-done((bf16[48,48]{1,0:T(8,128)(2,1)S(1)}, bf16[48,48]{1,0:T(8,128)(2,1)}, u32[]{:S(2)}) %copy-start.16) | copy-done | bytes 4632
  14.8 0.0 copy-start.17
  14.8 0.7 %copy-done.17 = s32[4,2,64]{2,1,0:T(2,128)S(1)} copy-done((s32[4,2,64]{2,1,0:T(2,128)S(1)}, s32[4,2,64]{2,1,0:T(2,128)}, u32[]{:S(2)}) %copy-start.17) | copy-done | bytes 2072
  15.5 0.0 copy-start.18
  15.5 0.7 %copy-done.18 = s32[4]{0:T(128)S(1)} copy-done((s32[4]{0:T(128)S(1)}, s32[4]{0:T(128)}, u32[]{:S(2)}) %copy-start.18) | copy-done | bytes 40
  16.2 30.8 %shard_map.190 = f32[3,32,1024]{2,1,0:T(8,128)S(1)} custom-call(s32[4]{0:T(128)S(1)} %copy-done.18, bf16[4,3,64,1024]{3,2,1,0:T(8,128)(2,1)} %photos.1, s32[4,2,64]{2,1,0:T(2,128)S(1)} %copy-done.17, bf16[128,256]{1,0:T(8,128)(2,1)S(1)} %copy-done.10, bf16[512,128]{1,0:T(8,128)(2,1)S(1)} %copy-done.7, bf16[128,128]{1,0:T(8,128)(2,1)S(1)} %copy-done.13, ...), custom_call_target="tpu_custom_call" | custom-call | tf_op jit(solution)/shard_map/pallas_call | solution.py:378
  47.0 0.7 %copy.22 = f32[3,32,1024]{2,1,0:T(8,128)} copy(f32[3,32,1024]{2,1,0:T(8,128)S(1)} %shard_map.190) | data formatting | bytes 786432
Async XLA Ops:
  0.0 1.2 %copy-start = (bf16[3,384,384]{2,1,0:T(8,128)(2,1)S(1)}, bf16[3,384,384]{2,1,0:T(8,128)(2,1)}, u32[]{:S(2)}) copy-start(bf16[3,384,384]{2,1,0:T(8,128)(2,1)} %constant.37.clone.h35) | copy-start | bytes 2654212
  1.2 1.0 %copy-start.1 = (bf16[384,640]{1,0:T(8,128)(2,1)S(1)}, bf16[384,640]{1,0:T(8,128)(2,1)}, u32[]{:S(2)}) copy-start(bf16[384,640]{1,0:T(8,128)(2,1)} %constant.42.clone.ec1) | copy-start | bytes 1474564
  2.2 0.9 %copy-start.2 = (bf16[256,512]{1,0:T(8,128)(2,1)S(1)}, bf16[256,512]{1,0:T(8,128)(2,1)}, u32[]{:S(2)}) copy-start(bf16[256,512]{1,0:T(8,128)(2,1)} %constant.47.clone.d0) | copy-start | bytes 786436
  3.1 0.9 %copy-start.3 = (bf16[3,64,640]{2,1,0:T(8,128)(2,1)S(1)}, bf16[3,64,640]{2,1,0:T(8,128)(2,1)}, u32[]{:S(2)}) copy-start(bf16[3,64,640]{2,1,0:T(8,128)(2,1)} %constant.48.clone.lb) | copy-start | bytes 737284
  4.1 0.9 %copy-start.4 = (bf16[256,384]{1,0:T(8,128)(2,1)S(1)}, bf16[256,384]{1,0:T(8,128)(2,1)}, u32[]{:S(2)}) copy-start(bf16[256,384]{1,0:T(8,128)(2,1)} %constant.43.clone.ec2) | copy-start | bytes 589828
  5.0 0.9 %copy-start.5 = (bf16[384,192]{1,0:T(8,128)(2,1)S(1)}, bf16[384,192]{1,0:T(8,128)(2,1)}, u32[]{:S(2)}) copy-start(bf16[384,192]{1,0:T(8,128)(2,1)} %constant.38.clone.er1) | copy-start | bytes 442372
  5.9 0.9 %copy-start.6 = (bf16[256,256]{1,0:T(8,128)(2,1)S(1)}, bf16[256,256]{1,0:T(8,128)(2,1)}, u32[]{:S(2)}) copy-start(bf16[256,256]{1,0:T(8,128)(2,1)} %constant.46.clone.e0) | copy-start | bytes 393220
  6.9 0.9 %copy-start.7 = (bf16[512,128]{1,0:T(8,128)(2,1)S(1)}, bf16[512,128]{1,0:T(8,128)(2,1)}, u32[]{:S(2)}) copy-start(bf16[512,128]{1,0:T(8,128)(2,1)} %constant.35.clone.wred) | copy-start | bytes 393220
  7.8 0.9 %copy-start.8 = (bf16[3,64,256]{2,1,0:T(8,128)(2,1)S(1)}, bf16[3,64,256]{2,1,0:T(8,128)(2,1)}, u32[]{:S(2)}) copy-start(bf16[3,64,256]{2,1,0:T(8,128)(2,1)} %constant.49.clone.lb5) | copy-start | bytes 294916
  8.7 0.8 %copy-start.9 = (bf16[128,256]{1,0:T(8,128)(2,1)S(1)}, bf16[128,256]{1,0:T(8,128)(2,1)}, u32[]{:S(2)}) copy-start(bf16[128,256]{1,0:T(8,128)(2,1)} %constant.44.clone.ec3) | copy-start | bytes 196612
  9.5 0.8 %copy-start.10 = (bf16[128,256]{1,0:T(8,128)(2,1)S(1)}, bf16[128,256]{1,0:T(8,128)(2,1)}, u32[]{:S(2)}) copy-start(bf16[128,256]{1,0:T(8,128)(2,1)} %constant.34.clone.v1) | copy-start | bytes 196612
  10.3 0.8 %copy-start.11 = (bf16[192,96]{1,0:T(8,128)(2,1)S(1)}, bf16[192,96]{1,0:T(8,128)(2,1)}, u32[]{:S(2)}) copy-start(bf16[192,96]{1,0:T(8,128)(2,1)} %constant.39.clone.er2) | copy-start | bytes 110596
  11.1 0.8 %copy-start.12 = (bf16[128,128]{1,0:T(8,128)(2,1)S(1)}, bf16[128,128]{1,0:T(8,128)(2,1)}, u32[]{:S(2)}) copy-start(bf16[128,128]{1,0:T(8,128)(2,1)} %constant.45.clone.ec4) | copy-start | bytes 98308
  11.9 0.8 %copy-start.13 = (bf16[128,128]{1,0:T(8,128)(2,1)S(1)}, bf16[128,128]{1,0:T(8,128)(2,1)}, u32[]{:S(2)}) copy-start(bf16[128,128]{1,0:T(8,128)(2,1)} %constant.36.clone.v25) | copy-start | bytes 98308
  12.6 0.7 %copy-start.14 = (bf16[96,48]{1,0:T(8,128)(2,1)S(1)}, bf16[96,48]{1,0:T(8,128)(2,1)}, u32[]{:S(2)}) copy-start(bf16[96,48]{1,0:T(8,128)(2,1)} %constant.40.clone.er3) | copy-start | bytes 27652
  13.4 0.7 %copy-start.15 = (f32[8,640]{1,0:T(8,128)S(1)}, f32[8,640]{1,0:T(8,128)}, u32[]{:S(2)}) copy-start(f32[8,640]{1,0:T(8,128)} %constant.50.clone.pm) | copy-start | bytes 61444
  14.1 0.7 %copy-start.16 = (bf16[48,48]{1,0:T(8,128)(2,1)S(1)}, bf16[48,48]{1,0:T(8,128)(2,1)}, u32[]{:S(2)}) copy-start(bf16[48,48]{1,0:T(8,128)(2,1)} %constant.41.clone.er4) | copy-start | bytes 13828
  14.8 0.7 %copy-start.17 = (s32[4,2,64]{2,1,0:T(2,128)S(1)}, s32[4,2,64]{2,1,0:T(2,128)}, u32[]{:S(2)}) copy-start(s32[4,2,64]{2,1,0:T(2,128)} %seams.1) | copy-start | bytes 6148
  15.5 0.7 %copy-start.18 = (s32[4]{0:T(128)S(1)}, s32[4]{0:T(128)}, u32[]{:S(2)}) copy-start(s32[4]{0:T(128)} %offsets.1) | copy-start | bytes 52

commit v2 on v1

--- a/solution.py
+++ b/solution.py
@@ -159,11 +159,38 @@
     return hi, (x - hi.astype(F32)).astype(BF)
 
 
-def kernel(n_strip, n_lvl, offsets, photos, seams, v1, wred, v25, h35, er1, er2, er3, er4, ec1, ec2, ec3, ec4, e0, d0, lb, lb5, pm,
-           out, s0, s1, tm, g1, ys, y2, c1h, c1l, send2, sendd, keep, relay, r1, r2, r3,
-           halo_send, halo_recv, m1_send, m1_recv, m2_send, m2_recv, m3_send, m3_recv):
+def kernel(n_strip, n_lvl, offsets, photos_in, seams, *refs):
+    given, out, held, rest = refs[: len(NAMES)], refs[len(NAMES)], refs[len(NAMES) + 1 : 2 * len(NAMES) + 1], refs[2 * len(NAMES) + 1 :]
+    body(n_strip, n_lvl, offsets, photos_in, seams, dict(zip(NAMES, given)), out, dict(zip(NAMES, held)), *rest)
+
+
+def body(n_strip, n_lvl, offsets, photos_in, seams, given, out, held, load, photos, s0, s1, tm, g1, ys, y2, c1h, c1l, send2, sendd, keep, relay, r1, r2, r3,
+         halo_send, halo_recv, m1_send, m1_recv, m2_send, m2_recv, m3_send, m3_recv):
     x = lax.axis_index("strip")
     me = lax.axis_index("lvl")
+    edge = jnp.where(me == 0, 0, jnp.where(me == n_lvl - 1, 2, 1))
+    waits = {}
+
+    def fetch(name, src, dst):
+        copy = pltpu.make_async_copy(src, dst, load.at[len(waits)])
+        copy.start()
+        waits[name] = copy
+
+    def ready(name):
+        if waits[name] is not None:
+            waits[name].wait()
+            waits[name] = None
+
+    def const(name):
+        ready(name)
+        return held[name]
+
+    fetch("v1", given["v1"], held["v1"])
+    for ch in range(3):
+        fetch(ch, photos_in.at[:, ch], photos.at[:, ch])
+    for name in NAMES[1:]:
+        fetch(name, given[name].at[edge] if name == "h35" else given[name], held[name])
+
     right, left = lax.rem(me + 1, n_lvl), lax.rem(me + n_lvl - 1, n_lvl)
     up, down = lax.rem(x + 1, n_strip), lax.rem(x + n_strip - 1, n_strip)
     barrier = pltpu.get_barrier_semaphore()
@@ -188,7 +215,9 @@
     def rows_of(ch, start, width):
         return photos[:, ch, :, start : start + width].reshape(256, width)
 
-    lead = v1[...]
+    lead = const("v1")[...]
+    for ch in range(3):
+        ready(ch)
     for start in (0, N - 128):
         for ch in range(3):
             tm[ch, :, HALO + start : HALO + start + 128] = dot(lead, rows_of(ch, start, 128)).astype(BF)
@@ -211,6 +240,8 @@
         m = jnp.where(mask_tile(start), 1.0, 0.0).astype(BF)
         tm[3, :, start : start + 128] = dot(lead, m).astype(BF)
 
+    wred = const("wred")
+
     def g1_tile(j):
         a, b = max(0, 2 * j - 1), min(10, 2 * j + 3)
         w = wred[128 * (a - 2 * j + 1) : 128 * (b - 2 * j + 1), :]
@@ -237,27 +268,28 @@
         g1_tile(j)
 
     for ch in range(4):
-        ys[128 * ch : 128 * ch + 128, :] = dot(v25[...], g1[128 * ch : 128 * ch + 128, :]).astype(BF)
+        ys[128 * ch : 128 * ch + 128, :] = dot(const("v25")[...], g1[128 * ch : 128 * ch + 128, :]).astype(BF)
     col = lax.broadcasted_iota(jnp.int32, (1, 384), 1) - 32 + me * (N // 4)
     inside = (col >= 0) & (col < n_lvl * (N // 4))
     for j, a, b in ((0, 0, 3), (1, 1, 5), (2, 3, 5)):
         w = wred[128 * (a - 2 * j + 1) : 128 * (b - 2 * j + 1), :]
         val = dot(ys[:, 128 * a : 128 * b], w)
         y2[:, 128 * j : 128 * j + 128] = jnp.where(inside[:, 128 * j : 128 * j + 128], val, 0.0).astype(BF)
-    edge = jnp.where(me == 0, 0, jnp.where(me == n_lvl - 1, 2, 1))
     y = y2[...].reshape(4, 128, 384)
     g2 = y[:, 0:64].reshape(256, 384)
-    y35 = dot(y[:, 64:128].reshape(256, 384), h35[edge]).astype(BF).reshape(4, 64, 384)
+    y35 = dot(y[:, 64:128].reshape(256, 384), const("h35")[...]).astype(BF).reshape(4, 64, 384)
     g3 = y35[:, 0:32, 0:256].reshape(128, 256)
     g4 = y35[:, 32:48, 256:384].reshape(64, 128)
     g5 = y35[:, 48:64, 256:384].reshape(64, 128)
     gs = {1: g1[...], 2: g2, 3: g3, 4: g4, 5: g5}
 
     weighted = {}
-    for k, er, ec, color in ((4, er4, ec4, 48), (3, er3, ec3, 48), (2, er2, ec2, 96), (1, er1, ec1, 192)):
+    er = {k: const(f"er{k}") for k in (1, 2, 3, 4)}
+    ec = {k: const(f"ec{k}") for k in (1, 2, 3, 4)}
+    for k, color in ((4, 48), (3, 48), (2, 96), (1, 192)):
         tall = 4 * ROWS[k]
-        u_hi, u_lo = halves(dot(er[...], gs[k + 1][0:color]))
-        expanded = dot(jnp.concatenate([u_hi, u_lo], axis=0), ec[...])
+        u_hi, u_lo = halves(dot(er[k][...], gs[k + 1][0:color]))
+        expanded = dot(jnp.concatenate([u_hi, u_lo], axis=0), ec[k][...])
         half = 3 * tall
         g = gs[k].astype(F32)
         detail = g[0:half] - (expanded[0:half] + expanded[half:])
@@ -266,6 +298,7 @@
     g = g5.astype(F32)
     weighted[5] = [(g[48:64] * g[16 * ch : 16 * ch + 16]).astype(BF) for ch in range(3)]
 
+    pm, lb, lb5 = const("pm"), const("lb"), const("lb5")
     places = [offsets[p].astype(F32) for p in range(4)]
 
     def by_photo(which):
@@ -291,9 +324,9 @@
         placed[k] = jnp.concatenate(parts, axis=0)
 
     total = placed[5]
-    for k, ec in ((4, ec4), (3, ec3), (2, ec2), (1, ec1)):
+    for k in (4, 3, 2, 1):
         hi, lo = halves(total)
-        got = dot(jnp.concatenate([hi, lo], axis=0), ec[...])
+        got = dot(jnp.concatenate([hi, lo], axis=0), ec[k][...])
         col = lax.broadcasted_iota(jnp.int32, (1, PAD[k]), 1) - (HALO >> k) + me * (N >> k)
         ok = (col >= 0) & (col < n_lvl * (N >> k))
         total = placed[k] + jnp.where(ok, got[0:192] + got[192:384], 0.0)
@@ -322,6 +355,7 @@
         return copy
 
     order = (0, 2, 1, 3)
+    e0, d0 = const("e0"), const("d0")
     first, direct, second = {}, {}, {}
 
     def pass_on(t):
@@ -373,14 +407,19 @@
 
     def per_device(photos, seams, offsets):
         vm = pl.BlockSpec(memory_space=pltpu.VMEM)
+        far = pl.BlockSpec(memory_space=pltpu.HBM)
+        given = [jnp.asarray(table[name]) for name in NAMES]
         dma = pltpu.SemaphoreType.DMA
         tile = (4, 96, 256)
         return pl.pallas_call(
             functools.partial(kernel, n_strip, n_lvl),
             out_shape=jax.ShapeDtypeStruct((3, 32, N), F32),
-            in_specs=[pl.BlockSpec(memory_space=pltpu.SMEM)] + [vm] * (2 + len(NAMES)),
+            in_specs=[pl.BlockSpec(memory_space=pltpu.SMEM), far, vm] + [far] * len(NAMES),
             out_specs=vm,
             scratch_shapes=[
+                *[pltpu.VMEM(a.shape[1:] if name == "h35" else a.shape, a.dtype) for name, a in zip(NAMES, given)],
+                dma((len(NAMES) + 3,)),
+                pltpu.VMEM((4, 3, 64, N), BF),
                 pltpu.VMEM((256, 128), F32),
                 pltpu.VMEM((256, 128), F32),
                 pltpu.VMEM((4, 128, 1280), BF),
@@ -398,8 +437,8 @@
                 pltpu.VMEM(tile, BF),
                 dma((2,)), dma((2,)), dma((4,)), dma((4,)), dma((4,)), dma((4,)), dma((4,)), dma((4,)),
             ],
-            compiler_params=pltpu.CompilerParams(collective_id=0, has_side_effects=True, vmem_limit_bytes=50 << 20),
-        )(offsets, photos, seams, *[jnp.asarray(table[name]) for name in NAMES])
+            compiler_params=pltpu.CompilerParams(collective_id=0, has_side_effects=True),
+        )(offsets, photos, seams, *given)
 
     placed = (P("strip", None, None, "lvl"), P("strip", None, None), P("strip"))
     return jax.shard_map(

time: 48.6 us -> 33.8 us (0.70)
  local copies, waits for them, and re-layouts: 16.9 us -> 1.77 us
  Pallas kernels: 30.8 us -> 31.6 us
    unnamed x39 -> x1, local copies, waits for them, and re-layouts: 16.9 us -> 1.77 us
    pallas_call x1, Pallas kernels: 30.8 us -> 31.6 us  [per_device(): pl.pallas_call(functools.partial(kernel, n_strip, n_lvl), out_shape=jax.S...]
where the time goes in v2:
time: 33.8 us; the launch traced here: 33.4 us
  Pallas kernels  31.6 us (93%)
  local copies, waits for them, and re-layouts  1.77 us (5%)
    pallas_call x1, Pallas kernels, per_device(): pl.pallas_call(functools.partial(kernel, n_strip, n_lvl), out_shape=jax.S...  31.6 us
    unnamed x1, local copies, waits for them, and re-layouts  1.77 us

profile of v2, /device:TPU:2, one launch (start us, length us, event | category | flops | bytes accessed | tf_op | source)
XLA Modules:
  0.0 33.4 jit_solution(271093318079462238)
XLA Ops:
  0.0 31.6 %shard_map.190 = f32[3,32,1024]{2,1,0:T(8,128)} custom-call(s32[4]{0:T(128)} %offsets.1, bf16[4,3,64,1024]{3,2,1,0:T(8,128)(2,1)} %photos_in.1, s32[4,2,64]{2,1,0:T(2,128)} %seams.1, bf16[128,256]{1,0:T(8,128)(2,1)} %constant.34.clone.refs_0_, bf16[512,128]{1,0:T(8,128)(2,1)} %constant.35.clone.refs_1_, bf16[128,128]{1,0:T(8,128)(2,1)} %constant.36.clone.refs_2_, ...), custom_call_target="tpu_custom_call" | custom-call | tf_op jit(solution)/shard_map/pallas_call | solution.py:414
  31.6 1.8 %copy.22 = f32[3,32,1024]{2,1,0:T(8,128)} copy(f32[3,32,1024]{2,1,0:T(8,128)} %shard_map.190) | data formatting | bytes 786432

commit v3 on v2

--- a/solution.py
+++ b/solution.py
@@ -109,7 +109,10 @@
         m = np.zeros((PAD[k + 1], PAD[k]))
         at = 80 if k == 4 else 0
         m[at : at + WIDE[k + 1], : WIDE[k]] = expand_rows(WIDE[k + 1]).T
-        c[f"ec{k}"] = bf(m)
+        if k == 1:
+            c["ec1a"], c["ec1b"] = bf(m[0:256, 0:384]), bf(m[128:384, 384:640])
+        else:
+            c[f"ec{k}"] = bf(m)
     e0 = np.zeros((256, 256))
     for col in range(256):
         i = 64 + col // 2
@@ -118,8 +121,8 @@
         else:
             e0[i, col], e0[i + 1, col] = 0.5, 0.5
     c["e0"] = bf(e0)
-    er0 = -blocks(expand_rows(32), 4)
-    c["d0"] = bf(np.concatenate([np.eye(256), er0, er0], axis=1))
+    er0 = blocks(expand_rows(32), 4)
+    c["d0"] = bf(np.concatenate([er0, er0], axis=1))
     hi = np.zeros((3, 64, 640))
     lo = np.zeros((3, 64, 640))
     for first in range(3):
@@ -147,7 +150,7 @@
     return c
 
 
-NAMES = ("v1", "wred", "v25", "h35", "er1", "er2", "er3", "er4", "ec1", "ec2", "ec3", "ec4", "e0", "d0", "lb", "lb5", "pm")
+NAMES = ("v1", "wred", "v25", "h35", "er1", "er2", "er3", "er4", "ec1a", "ec1b", "ec2", "ec3", "ec4", "e0", "d0", "lb", "lb5", "pm")
 
 
 def dot(a, b):
@@ -159,58 +162,46 @@
     return hi, (x - hi.astype(F32)).astype(BF)
 
 
-def kernel(n_strip, n_lvl, offsets, photos_in, seams, *refs):
-    given, out, held, rest = refs[: len(NAMES)], refs[len(NAMES)], refs[len(NAMES) + 1 : 2 * len(NAMES) + 1], refs[2 * len(NAMES) + 1 :]
-    body(n_strip, n_lvl, offsets, photos_in, seams, dict(zip(NAMES, given)), out, dict(zip(NAMES, held)), *rest)
-
-
-def body(n_strip, n_lvl, offsets, photos_in, seams, given, out, held, load, photos, s0, s1, tm, g1, ys, y2, c1h, c1l, send2, sendd, keep, relay, r1, r2, r3,
+def kernel(n_strip, n_lvl, offsets_in, photos_in, seams_in, *refs):
+    n = len(NAMES)
+    given, (out, r2, r3), held, rest = refs[:n], refs[n : n + 3], refs[n + 3 : 2 * n + 3], refs[2 * n + 3 :]
+    body(n_strip, n_lvl, offsets_in, photos_in, seams_in, dict(zip(NAMES, given)), out, r2, r3, dict(zip(NAMES, held)), *rest)
+
+
+def body(n_strip, n_lvl, offsets_in, photos_in, seams_in, given, out, r2, r3, held, load, photos, offsets, seams, s0, s1, tm, g1, ys, y2, bands,
+         c1h, c1l, send2, sendd, keep, relay, r1, own, own_sem,
          halo_send, halo_recv, m1_send, m1_recv, m2_send, m2_recv, m3_send, m3_recv):
     x = lax.axis_index("strip")
     me = lax.axis_index("lvl")
-    edge = jnp.where(me == 0, 0, jnp.where(me == n_lvl - 1, 2, 1))
-    waits = {}
-
-    def fetch(name, src, dst):
-        copy = pltpu.make_async_copy(src, dst, load.at[len(waits)])
-        copy.start()
-        waits[name] = copy
-
-    def ready(name):
-        if waits[name] is not None:
-            waits[name].wait()
-            waits[name] = None
-
-    def const(name):
-        ready(name)
-        return held[name]
-
-    fetch("v1", given["v1"], held["v1"])
-    for ch in range(3):
-        fetch(ch, photos_in.at[:, ch], photos.at[:, ch])
-    for name in NAMES[1:]:
-        fetch(name, given[name].at[edge] if name == "h35" else given[name], held[name])
-
     right, left = lax.rem(me + 1, n_lvl), lax.rem(me + n_lvl - 1, n_lvl)
     up, down = lax.rem(x + 1, n_strip), lax.rem(x + n_strip - 1, n_strip)
     barrier = pltpu.get_barrier_semaphore()
     for target in ({"lvl": left}, {"lvl": right}, {"strip": up}, {"strip": down}):
         pl.semaphore_signal(barrier, inc=1, device_id=target, device_id_type=MESH)
-
-    r_i = lax.broadcasted_iota(jnp.int32, (64, 64), 0)
-    c_i = lax.broadcasted_iota(jnp.int32, (64, 64), 1)
-    eye = r_i == c_i
-    for p in range(4):
-        for e, dst in ((0, s0), (1, s1)):
-            line = seams[p, e : e + 1, :].astype(F32)
-            col = jnp.sum(jnp.where(eye, line, 0.0), axis=1, keepdims=True)
-            dst[64 * p : 64 * p + 64, :] = jnp.broadcast_to(col, (64, 128))
-
-    first_col = (me * N).astype(F32)
-
-    def mask_tile(start):
-        col = lax.broadcasted_iota(jnp.int32, (256, 128), 1).astype(F32) + (first_col + (start - HALO))
-        return (col >= s0[...]) & (col < s1[...])
+    edge = jnp.where(me == 0, 0, jnp.where(me == n_lvl - 1, 2, 1))
+    waits = {}
+
+    def fetch(name, src, dst):
+        copy = pltpu.make_async_copy(src, dst, load.at[len(waits)])
+        copy.start()
+        waits[name] = copy
+
+    def ready(name):
+        if waits[name] is not None:
+            waits[name].wait()
+            waits[name] = None
+
+    def const(name):
+        ready(name)
+        return held[name]
+
+    fetch("seams", seams_in, seams)
+    fetch("v1", given["v1"], held["v1"])
+    for ch in range(3):
+        fetch(ch, photos_in.at[:, ch], photos.at[:, ch])
+    fetch("offsets", offsets_in, offsets)
+    for name in NAMES[1:]:
+        fetch(name, given[name].at[edge] if name == "h35" else given[name], held[name])
 
     def rows_of(ch, start, width):
         return photos[:, ch, :, start : start + width].reshape(256, width)
@@ -234,11 +225,28 @@
         )
         copy.start()
         halo.append(copy)
+    r_i = lax.broadcasted_iota(jnp.int32, (64, 64), 0)
+    c_i = lax.broadcasted_iota(jnp.int32, (64, 64), 1)
+    eye = r_i == c_i
+    ready("seams")
+    for p in range(4):
+        for e, dst in ((0, s0), (1, s1)):
+            line = seams[p, e : e + 1, :].astype(F32)
+            col = jnp.sum(jnp.where(eye, line, 0.0), axis=1, keepdims=True)
+            dst[64 * p : 64 * p + 64, :] = jnp.broadcast_to(col, (64, 128))
+
+    first_col = (me * N).astype(F32)
+
+    def mask_tile(start):
+        col = lax.broadcasted_iota(jnp.int32, (256, 128), 1).astype(F32) + (first_col + (start - HALO))
+        a, b = s0[...], s1[...]
+        return jnp.concatenate([(c >= a) & (c < b) for c in (col, col + 128.0)], axis=1)
+
     for ch in range(3):
         tm[ch, :, 256 : N] = dot(lead, rows_of(ch, 128, N - 256)).astype(BF)
-    for start in range(0, N + 256, 128):
+    for start in range(0, N + 256, 256):
         m = jnp.where(mask_tile(start), 1.0, 0.0).astype(BF)
-        tm[3, :, start : start + 128] = dot(lead, m).astype(BF)
+        tm[3, :, start : start + 256] = dot(lead, m).astype(BF)
 
     wred = const("wred")
 
@@ -253,17 +261,25 @@
 
     for j in (1, 2, 3):
         g1_tile(j)
+    e0, d0 = const("e0"), const("d0")
+
+    def band(t, ch):
+        cols = slice(128 * t, 128 * t + 256)
+        u_hi, u_lo = halves(dot(g1[128 * ch : 128 * ch + 128, cols], e0[...]))
+        away = dot(d0[...], jnp.concatenate([u_hi, u_lo], axis=0))
+        detail = rows_of(ch, 256 * t, 256).astype(F32) - away
+        bands[ch, :, 256 * t : 256 * t + 256] = jnp.where(mask_tile(HALO + 256 * t), detail, 0.0).astype(BF)
+
+    for t in (1, 2):
+        for ch in range(3):
+            band(t, ch)
+    for name in NAMES:
+        ready(name)
+    ready("offsets")
     for copy in halo:
         copy.wait()
-
-    @pl.when(me == 0)
-    def _():
-        tm[0:3, :, 0:128] = jnp.zeros((3, 128, 128), BF)
-
-    @pl.when(me == n_lvl - 1)
-    def _():
-        tm[0:3, :, N + 128 : N + 256] = jnp.zeros((3, 128, 128), BF)
-
+    for at, outer in ((0, 0), (N + 128, n_lvl - 1)):
+        tm[0:3, :, at : at + 128] = jnp.where(me == outer, jnp.zeros((), BF), tm[0:3, :, at : at + 128])
     for j in (0, 4):
         g1_tile(j)
 
@@ -275,26 +291,34 @@
         w = wred[128 * (a - 2 * j + 1) : 128 * (b - 2 * j + 1), :]
         val = dot(ys[:, 128 * a : 128 * b], w)
         y2[:, 128 * j : 128 * j + 128] = jnp.where(inside[:, 128 * j : 128 * j + 128], val, 0.0).astype(BF)
+    band(0, 0)
     y = y2[...].reshape(4, 128, 384)
     g2 = y[:, 0:64].reshape(256, 384)
     y35 = dot(y[:, 64:128].reshape(256, 384), const("h35")[...]).astype(BF).reshape(4, 64, 384)
     g3 = y35[:, 0:32, 0:256].reshape(128, 256)
     g4 = y35[:, 32:48, 256:384].reshape(64, 128)
     g5 = y35[:, 48:64, 256:384].reshape(64, 128)
+    band(0, 1)
     gs = {1: g1[...], 2: g2, 3: g3, 4: g4, 5: g5}
 
     weighted = {}
     er = {k: const(f"er{k}") for k in (1, 2, 3, 4)}
-    ec = {k: const(f"ec{k}") for k in (1, 2, 3, 4)}
+
+    def widen(k, field):
+        if k == 1:
+            return jnp.concatenate([dot(field[:, 0:256], held["ec1a"][...]), dot(field[:, 128:384], held["ec1b"][...])], axis=1)
+        return dot(field, held[f"ec{k}"][...])
+
     for k, color in ((4, 48), (3, 48), (2, 96), (1, 192)):
         tall = 4 * ROWS[k]
         u_hi, u_lo = halves(dot(er[k][...], gs[k + 1][0:color]))
-        expanded = dot(jnp.concatenate([u_hi, u_lo], axis=0), ec[k][...])
+        expanded = widen(k, jnp.concatenate([u_hi, u_lo], axis=0))
         half = 3 * tall
         g = gs[k].astype(F32)
         detail = g[0:half] - (expanded[0:half] + expanded[half:])
         m = g[half:]
         weighted[k] = [(m * detail[ch * tall : ch * tall + tall]).astype(BF) for ch in range(3)]
+    band(0, 2)
     g = g5.astype(F32)
     weighted[5] = [(g[48:64] * g[16 * ch : 16 * ch + 16]).astype(BF) for ch in range(3)]
 
@@ -310,6 +334,7 @@
     spot = by_photo(pm[0:1, :])
     table = sum(jnp.where(spot == float(o), lb[o].astype(F32), 0.0) for o in range(3)).astype(BF)
     fine = sum(jnp.where(spot[:, 384:] == float(o), lb5[o].astype(F32), 0.0) for o in range(3)).astype(BF)
+    band(3, 0)
     placed = {}
     for k in (5, 4, 3, 2, 1):
         s = 128 * (k - 1)
@@ -323,13 +348,16 @@
             parts.append(got[0:64] + got[64:128] if k >= 4 else got)
         placed[k] = jnp.concatenate(parts, axis=0)
 
+    band(3, 1)
+
     total = placed[5]
     for k in (4, 3, 2, 1):
         hi, lo = halves(total)
-        got = dot(jnp.concatenate([hi, lo], axis=0), ec[k][...])
+        got = widen(k, jnp.concatenate([hi, lo], axis=0))
         col = lax.broadcasted_iota(jnp.int32, (1, PAD[k]), 1) - (HALO >> k) + me * (N >> k)
         ok = (col >= 0) & (col < n_lvl * (N >> k))
         total = placed[k] + jnp.where(ok, got[0:192] + got[192:384], 0.0)
+    band(3, 2)
     hi, lo = halves(total)
     c1h[...] = hi
     c1l[...] = lo
@@ -355,46 +383,40 @@
         return copy
 
     order = (0, 2, 1, 3)
-    e0, d0 = const("e0"), const("d0")
-    first, direct, second = {}, {}, {}
+    first, direct, second, done = {}, {}, {}, {}
 
     def pass_on(t):
         first[t].wait_recv()
         relay[t] = (keep[t] + r1[t].astype(F32)).astype(BF)
-        second[t] = remote(relay.at[t], r2.at[t], m2_send.at[t], m2_recv.at[t], up if t < 2 else down)
+        cols = slice(256 * t, 256 * t + 256)
+        second[t] = remote(relay.at[t], r2.at[:, :, cols], m2_send.at[t], m2_recv.at[t], up if t < 2 else down)
 
     for i, t in enumerate(order):
         cols = slice(128 * t, 128 * t + 256)
-        lhs = jnp.concatenate([g1[0:384, cols], c1h[:, cols], c1l[:, cols]], axis=0)
-        wide = dot(lhs, e0[...])
-        u_hi, u_lo = halves(wide[0:384])
-        b_hi, b_lo = halves(wide[384:576] + wide[576:768])
-        inside = jnp.concatenate([mask_tile(HALO + 256 * t), mask_tile(HALO + 256 * t + 128)], axis=1)
+        wide = dot(jnp.concatenate([c1h[:, cols], c1l[:, cols]], axis=0), e0[...])
+        b_hi, b_lo = halves(wide[0:192] + wide[192:384])
+        cols = slice(256 * t, 256 * t + 256)
         for ch in range(3):
-            r = slice(128 * ch, 128 * ch + 128)
-            rhs = jnp.concatenate([rows_of(ch, 256 * t, 256), u_hi[r], u_lo[r]], axis=0)
-            band = jnp.where(inside, dot(d0[...], rhs), 0.0).astype(BF)
             r = slice(64 * ch, 64 * ch + 64)
-            got = dot(last, jnp.concatenate([band, b_hi[r], b_lo[r]], axis=0))
-            out[ch, :, 256 * t : 256 * t + 256] = got[0:32]
-            rr = slice(32 * ch, 32 * ch + 32)
-            send2[t, rr, :] = got[64:96].astype(BF)
+            got = dot(last, jnp.concatenate([bands[ch, :, cols], b_hi[r], b_lo[r]], axis=0))
+            own[t, ch] = got[0:32]
+            send2[t, ch] = got[64:96].astype(BF)
             via, away = (got[32:64], got[96:128]) if t < 2 else (got[96:128], got[32:64])
-            keep[t, rr, :] = via
-            sendd[t, rr, :] = away.astype(BF)
+            keep[t, ch] = via
+            sendd[t, ch] = away.astype(BF)
         forward, back = (up, down) if t < 2 else (down, up)
         first[t] = remote(send2.at[t], r1.at[t], m1_send.at[t], m1_recv.at[t], forward)
-        direct[t] = remote(sendd.at[t], r3.at[t], m3_send.at[t], m3_recv.at[t], back)
-        if i > 0:
-            pass_on(order[i - 1])
-    pass_on(order[-1])
+        direct[t] = remote(sendd.at[t], r3.at[:, :, cols], m3_send.at[t], m3_recv.at[t], back)
+        done[t] = pltpu.make_async_copy(own.at[t], out.at[:, :, cols], own_sem.at[t])
+        done[t].start()
+        if i == 3:
+            pass_on(order[0])
+    for t in order[1:]:
+        pass_on(t)
     for t in order:
+        done[t].wait()
         direct[t].wait_recv()
         second[t].wait_recv()
-        got = r2[t].astype(F32) + r3[t].astype(F32)
-        for ch in range(3):
-            c = slice(256 * t, 256 * t + 256)
-            out[ch, :, c] = out[ch, :, c] + got[32 * ch : 32 * ch + 32]
     for t in order:
         first[t].wait_send()
         direct[t].wait_send()
@@ -406,26 +428,29 @@
     table = constants()
 
     def per_device(photos, seams, offsets):
-        vm = pl.BlockSpec(memory_space=pltpu.VMEM)
         far = pl.BlockSpec(memory_space=pltpu.HBM)
         given = [jnp.asarray(table[name]) for name in NAMES]
         dma = pltpu.SemaphoreType.DMA
-        tile = (4, 96, 256)
-        return pl.pallas_call(
+        tile = (4, 3, 32, 256)
+        strip = (3, 32, N)
+        out, r2, r3 = pl.pallas_call(
             functools.partial(kernel, n_strip, n_lvl),
-            out_shape=jax.ShapeDtypeStruct((3, 32, N), F32),
-            in_specs=[pl.BlockSpec(memory_space=pltpu.SMEM), far, vm] + [far] * len(NAMES),
-            out_specs=vm,
+            out_shape=(jax.ShapeDtypeStruct(strip, F32), jax.ShapeDtypeStruct(strip, BF), jax.ShapeDtypeStruct(strip, BF)),
+            in_specs=[far] * (3 + len(NAMES)),
+            out_specs=(far, far, far),
             scratch_shapes=[
                 *[pltpu.VMEM(a.shape[1:] if name == "h35" else a.shape, a.dtype) for name, a in zip(NAMES, given)],
-                dma((len(NAMES) + 3,)),
+                dma((len(NAMES) + 5,)),
                 pltpu.VMEM((4, 3, 64, N), BF),
+                pltpu.SMEM((4,), jnp.int32),
+                pltpu.VMEM((4, 2, 64), jnp.int32),
                 pltpu.VMEM((256, 128), F32),
                 pltpu.VMEM((256, 128), F32),
                 pltpu.VMEM((4, 128, 1280), BF),
                 pltpu.VMEM((512, 640), BF),
                 pltpu.VMEM((512, 640), BF),
                 pltpu.VMEM((512, 384), BF),
+                pltpu.VMEM((3, 256, N), BF),
                 pltpu.VMEM((192, 640), BF),
                 pltpu.VMEM((192, 640), BF),
                 pltpu.VMEM(tile, BF),
@@ -433,12 +458,13 @@
                 pltpu.VMEM(tile, F32),
                 pltpu.VMEM(tile, BF),
                 pltpu.VMEM(tile, BF),
-                pltpu.VMEM(tile, BF),
-                pltpu.VMEM(tile, BF),
+                pltpu.VMEM(tile, F32),
+                dma((4,)),
                 dma((2,)), dma((2,)), dma((4,)), dma((4,)), dma((4,)), dma((4,)), dma((4,)), dma((4,)),
             ],
             compiler_params=pltpu.CompilerParams(collective_id=0, has_side_effects=True),
         )(offsets, photos, seams, *given)
+        return out + (r2.astype(F32) + r3.astype(F32))
 
     placed = (P("strip", None, None, "lvl"), P("strip", None, None), P("strip"))
     return jax.shard_map(

time: 33.8 us -> 27.6 us (0.82)
  Pallas kernels: 31.6 us -> 25.3 us
  other arithmetic: 0 us -> 1.96 us
  local copies, waits for them, and re-layouts: 1.77 us -> 0 us
    pallas_call x1, Pallas kernels: 31.6 us -> 25.3 us  [per_device(): pl.pallas_call(functools.partial(kernel, n_strip, n_lvl), out_shape=(jax....]
    add x0 -> x1, other arithmetic: none -> 1.96 us  [per_device(): return out + (r2.astype(F32) + r3.astype(F32))]
    unnamed x1 -> x0, local copies, waits for them, and re-layouts: 1.77 us -> none
where the time goes in v3:
time: 27.6 us; the launch traced here: 27.2 us
  Pallas kernels  25.3 us (92%)
  other arithmetic  1.96 us (7%)
    pallas_call x1, Pallas kernels, per_device(): pl.pallas_call(functools.partial(kernel, n_strip, n_lvl), out_shape=(jax....  25.3 us
    add x1, other arithmetic, per_device(): return out + (r2.astype(F32) + r3.astype(F32))  1.96 us

profile of v3, /device:TPU:2, one launch (start us, length us, event | category | flops | bytes accessed | tf_op | source)
XLA Modules:
  0.0 27.2 jit_solution(8046265141228558032)
XLA Ops:
  0.0 25.3 %shard_map.199 = (f32[3,32,1024]{2,1,0:T(8,128)}, bf16[3,32,1024]{2,1,0:T(8,128)(2,1)}, bf16[3,32,1024]{2,1,0:T(8,128)(2,1)}) custom-call(s32[4]{0:T(128)} %offsets_in.1, bf16[4,3,64,1024]{3,2,1,0:T(8,128)(2,1)} %photos_in.1, s32[4,2,64]{2,1,0:T(2,128)} %seams_in.1, bf16[128,256]{1,0:T(8,128)(2,1)} %constant.36.clone.refs_0_, ...), custom_call_target="tpu_custom_call" | custom-call | tf_op jit(solution)/shard_map/pallas_call | solution.py:436
  25.3 2.0 %add_add_fusion = f32[3,32,1024]{2,1,0:T(8,128)} fusion(f32[3,32,1024]{2,1,0:T(8,128)} %get-tuple-element.8, bf16[3,32,1024]{2,1,0:T(8,128)(2,1)} %get-tuple-element.10, bf16[3,32,1024]{2,1,0:T(8,128)(2,1)} %get-tuple-element.9), kind=kLoop, calls=%fused_computation | loop fusion | flops 393216 | bytes 1179648 | tf_op jit(solution)/shard_map/add | solution.py:467

commit v4 on v3

--- a/solution.py
+++ b/solution.py
@@ -122,6 +122,11 @@
             e0[i, col], e0[i + 1, col] = 0.5, 0.5
     c["e0"] = bf(e0)
     er0 = blocks(expand_rows(32), 4)
+    one = expand_rows(18)[2:34]
+    tall = np.zeros((96, 64))
+    for ch in range(3):
+        tall[32 * ch : 32 * ch + 32, 18 * ch : 18 * ch + 18] = one
+    c["tall"] = bf(np.concatenate([tall, tall], axis=1))
     c["d0"] = bf(np.concatenate([er0, er0], axis=1))
     hi = np.zeros((3, 64, 640))
     lo = np.zeros((3, 64, 640))
@@ -164,19 +169,19 @@
 
 def kernel(n_strip, n_lvl, offsets_in, photos_in, seams_in, *refs):
     n = len(NAMES)
-    given, (out, r2, r3), held, rest = refs[:n], refs[n : n + 3], refs[n + 3 : 2 * n + 3], refs[2 * n + 3 :]
-    body(n_strip, n_lvl, offsets_in, photos_in, seams_in, dict(zip(NAMES, given)), out, r2, r3, dict(zip(NAMES, held)), *rest)
-
-
-def body(n_strip, n_lvl, offsets_in, photos_in, seams_in, given, out, r2, r3, held, load, photos, offsets, seams, s0, s1, tm, g1, ys, y2, bands,
-         c1h, c1l, send2, sendd, keep, relay, r1, own, own_sem,
-         halo_send, halo_recv, m1_send, m1_recv, m2_send, m2_recv, m3_send, m3_recv):
+    given, outs, held, rest = refs[:n], refs[n : n + 5], refs[n + 5 : 2 * n + 5], refs[2 * n + 5 :]
+    body(n_strip, n_lvl, offsets_in, photos_in, seams_in, dict(zip(NAMES, given)), *outs, dict(zip(NAMES, held)), *rest)
+
+
+def body(n_strip, n_lvl, offsets_in, photos_in, seams_in, given, base_out, own_out, q1, q2, q3, held, load, photos, offsets, seams, s0, s1, tm, g1,
+         ys, y2, uh, ul, sent, got_in, base, low, lowo, out_sem,
+         halo_send, halo_recv, m_send, m_recv, n_send, n_recv):
     x = lax.axis_index("strip")
     me = lax.axis_index("lvl")
     right, left = lax.rem(me + 1, n_lvl), lax.rem(me + n_lvl - 1, n_lvl)
-    up, down = lax.rem(x + 1, n_strip), lax.rem(x + n_strip - 1, n_strip)
+    others = [lax.rem(x + j, n_strip) for j in range(n_strip)]
     barrier = pltpu.get_barrier_semaphore()
-    for target in ({"lvl": left}, {"lvl": right}, {"strip": up}, {"strip": down}):
+    for target in ({"lvl": left}, {"lvl": right}, {"strip": others[1]}, {"strip": others[2]}, {"strip": others[3]}):
         pl.semaphore_signal(barrier, inc=1, device_id=target, device_id_type=MESH)
     edge = jnp.where(me == 0, 0, jnp.where(me == n_lvl - 1, 2, 1))
     waits = {}
@@ -212,7 +217,7 @@
     for start in (0, N - 128):
         for ch in range(3):
             tm[ch, :, HALO + start : HALO + start + 128] = dot(lead, rows_of(ch, start, 128)).astype(BF)
-    pl.semaphore_wait(barrier, 4)
+    pl.semaphore_wait(barrier, 5)
     halo = []
     for i, (src, dst, target) in enumerate(((HALO, HALO + N, left), (N, 0, right))):
         copy = pltpu.make_async_remote_copy(
@@ -262,26 +267,56 @@
     for j in (1, 2, 3):
         g1_tile(j)
     e0, d0 = const("e0"), const("d0")
+    ready("offsets")
+    places = [offsets[p] for p in range(4)]
+
+    q = lax.broadcasted_iota(jnp.int32, (128, 256), 0)
+    lane = lax.broadcasted_iota(jnp.int32, (128, 256), 1)
+    where = jnp.where(lane < 64, places[0], jnp.where(lane < 128, places[1], jnp.where(lane < 192, places[2], places[3])))
+    put = jnp.where((((q >> 5) + x) & 3) * 32 + (q & 31) == where * 32 + (lane & 63), 1.0, 0.0).astype(BF)
+
+    def remote(src, dst, send, recv, target):
+        copy = pltpu.make_async_remote_copy(
+            src_ref=src, dst_ref=dst, send_sem=send, recv_sem=recv, device_id={"strip": target}, device_id_type=MESH
+        )
+        copy.start()
+        return copy
+
+    sends = []
+
+    def widened(t):
+        hi, lo = halves(dot(g1[0:384, 128 * t : 128 * t + 256], e0[...]))
+        uh[t], ul[t] = hi, lo
 
     def band(t, ch):
-        cols = slice(128 * t, 128 * t + 256)
-        u_hi, u_lo = halves(dot(g1[128 * ch : 128 * ch + 128, cols], e0[...]))
-        away = dot(d0[...], jnp.concatenate([u_hi, u_lo], axis=0))
+        r = slice(128 * ch, 128 * ch + 128)
+        away = dot(d0[...], jnp.concatenate([uh[t, r], ul[t, r]], axis=0))
         detail = rows_of(ch, 256 * t, 256).astype(F32) - away
-        bands[ch, :, 256 * t : 256 * t + 256] = jnp.where(mask_tile(HALO + 256 * t), detail, 0.0).astype(BF)
-
+        weighted_0 = jnp.where(mask_tile(HALO + 256 * t), detail, 0.0).astype(BF)
+        got = dot(put, weighted_0).astype(BF)
+        for j in range(4):
+            sent[t, j, ch] = got[32 * j : 32 * j + 32]
+
+    def send_band(t):
+        for j in (2, 1, 3):
+            sends.append(remote(sent.at[t, j], got_in.at[t, j], m_send.at[t, j - 1], m_recv.at[t, j - 1], others[j]))
+
+    widened(1)
+    widened(2)
     for t in (1, 2):
         for ch in range(3):
             band(t, ch)
+        send_band(t)
     for name in NAMES:
         ready(name)
-    ready("offsets")
     for copy in halo:
         copy.wait()
     for at, outer in ((0, 0), (N + 128, n_lvl - 1)):
         tm[0:3, :, at : at + 128] = jnp.where(me == outer, jnp.zeros((), BF), tm[0:3, :, at : at + 128])
     for j in (0, 4):
         g1_tile(j)
+    widened(0)
+    widened(3)
 
     for ch in range(4):
         ys[128 * ch : 128 * ch + 128, :] = dot(const("v25")[...], g1[128 * ch : 128 * ch + 128, :]).astype(BF)
@@ -319,16 +354,16 @@
         m = g[half:]
         weighted[k] = [(m * detail[ch * tall : ch * tall + tall]).astype(BF) for ch in range(3)]
     band(0, 2)
+    send_band(0)
     g = g5.astype(F32)
     weighted[5] = [(g[48:64] * g[16 * ch : 16 * ch + 16]).astype(BF) for ch in range(3)]
 
     pm, lb, lb5 = const("pm"), const("lb"), const("lb5")
-    places = [offsets[p].astype(F32) for p in range(4)]
 
     def by_photo(which):
         got = jnp.zeros(which.shape, F32)
         for p in range(4):
-            got = jnp.where(which == float(p), places[p], got)
+            got = jnp.where(which == float(p), places[p].astype(F32), got)
         return got
 
     spot = by_photo(pm[0:1, :])
@@ -349,7 +384,6 @@
         placed[k] = jnp.concatenate(parts, axis=0)
 
     band(3, 1)
-
     total = placed[5]
     for k in (4, 3, 2, 1):
         hi, lo = halves(total)
@@ -357,70 +391,48 @@
         col = lax.broadcasted_iota(jnp.int32, (1, PAD[k]), 1) - (HALO >> k) + me * (N >> k)
         ok = (col >= 0) & (col < n_lvl * (N >> k))
         total = placed[k] + jnp.where(ok, got[0:192] + got[192:384], 0.0)
-    band(3, 2)
+        if k == 4:
+            band(3, 2)
+            send_band(3)
+    q = lax.broadcasted_iota(jnp.int32, (256, 192), 0)
+    k = lax.broadcasted_iota(jnp.int32, (256, 192), 1)
+    rest = q & 63
+    ch = jnp.where(rest >= 18, 1, 0) + jnp.where(rest >= 36, 1, 0)
+    row = (((q >> 6) + x) & 3) * 16 + rest - 18 * ch - 1
+    pick = jnp.where((rest < 54) & (row == (k & 63)) & (ch == (k >> 6)), 1.0, 0.0).astype(BF)
     hi, lo = halves(total)
-    c1h[...] = hi
-    c1l[...] = lo
-
-    def strip_rows(width):
-        q = lax.broadcasted_iota(jnp.int32, (128, width), 0)
-        return ((q >> 5) + x) % 4 * 32 + (q & 31)
-
-    lane = lax.broadcasted_iota(jnp.int32, (128, 256), 1)
-    where = by_photo((lane >> 6).astype(F32)).astype(jnp.int32) * 32 + (lane & 63)
-    put = jnp.where(strip_rows(256) == where, 1.0, 0.0).astype(BF)
-    row = strip_rows(128)
-    d = (lax.broadcasted_iota(jnp.int32, (128, 128), 1) & 63) - (row >> 1)
-    even = jnp.where(d == 0, 0.75, jnp.where((d == 1) | (d == -1), 0.125, 0.0))
-    odd = jnp.where((d == 0) | (d == 1), 0.5, 0.0)
-    last = jnp.concatenate([put, jnp.where((row & 1) == 0, even, odd).astype(BF)], axis=1)
-
-    def remote(src, dst, send, recv, target):
-        copy = pltpu.make_async_remote_copy(
-            src_ref=src, dst_ref=dst, send_sem=send, recv_sem=recv, device_id={"strip": target}, device_id_type=MESH
-        )
-        copy.start()
-        return copy
-
-    order = (0, 2, 1, 3)
-    first, direct, second, done = {}, {}, {}, {}
-
-    def pass_on(t):
-        first[t].wait_recv()
-        relay[t] = (keep[t] + r1[t].astype(F32)).astype(BF)
+    got = dot(pick, hi)
+    lows = []
+    for j, there in ((2, q2), (1, q1), (3, q3)):
+        low[j - 1] = got[64 * j : 64 * j + 64].astype(BF)
+        lows.append(remote(low.at[j - 1], there, n_send.at[j - 1], n_recv.at[j - 1], others[j]))
+    lowo[...] = got[0:64] + dot(pick[0:64], lo)
+    copies = [pltpu.make_async_copy(lowo, own_out, out_sem.at[0])]
+    copies[0].start()
+
+    for copy in sends:
+        copy.wait_recv()
+    for t in range(4):
+        base[:, :, 256 * t : 256 * t + 256] = (sent[t, 0] + got_in[t, 1]) + (got_in[t, 2] + got_in[t, 3])
+    copies.append(pltpu.make_async_copy(base, base_out, out_sem.at[1]))
+    copies[1].start()
+    for copy in sends:
+        copy.wait_send()
+    for copy in lows:
+        copy.wait()
+    for copy in copies:
+        copy.wait()
+
+
+def finish(base, low, q1, q2, q3, e0, tall, out):
+    total = low[...] + (q2[...].astype(F32) + (q1[...].astype(F32) + q3[...].astype(F32)))
+    hi, lo = halves(total)
+    hi, lo = halves(dot(tall[...], jnp.concatenate([hi, lo], axis=0)))
+    for t in range(4):
+        cols = slice(128 * t, 128 * t + 256)
+        got = dot(jnp.concatenate([hi[:, cols], lo[:, cols]], axis=0), e0[...])
         cols = slice(256 * t, 256 * t + 256)
-        second[t] = remote(relay.at[t], r2.at[:, :, cols], m2_send.at[t], m2_recv.at[t], up if t < 2 else down)
-
-    for i, t in enumerate(order):
-        cols = slice(128 * t, 128 * t + 256)
-        wide = dot(jnp.concatenate([c1h[:, cols], c1l[:, cols]], axis=0), e0[...])
-        b_hi, b_lo = halves(wide[0:192] + wide[192:384])
-        cols = slice(256 * t, 256 * t + 256)
-        for ch in range(3):
-            r = slice(64 * ch, 64 * ch + 64)
-            got = dot(last, jnp.concatenate([bands[ch, :, cols], b_hi[r], b_lo[r]], axis=0))
-            own[t, ch] = got[0:32]
-            send2[t, ch] = got[64:96].astype(BF)
-            via, away = (got[32:64], got[96:128]) if t < 2 else (got[96:128], got[32:64])
-            keep[t, ch] = via
-            sendd[t, ch] = away.astype(BF)
-        forward, back = (up, down) if t < 2 else (down, up)
-        first[t] = remote(send2.at[t], r1.at[t], m1_send.at[t], m1_recv.at[t], forward)
-        direct[t] = remote(sendd.at[t], r3.at[:, :, cols], m3_send.at[t], m3_recv.at[t], back)
-        done[t] = pltpu.make_async_copy(own.at[t], out.at[:, :, cols], own_sem.at[t])
-        done[t].start()
-        if i == 3:
-            pass_on(order[0])
-    for t in order[1:]:
-        pass_on(t)
-    for t in order:
-        done[t].wait()
-        direct[t].wait_recv()
-        second[t].wait_recv()
-    for t in order:
-        first[t].wait_send()
-        direct[t].wait_send()
-        second[t].wait_send()
+        out[:, :, cols] = base[:, :, cols].astype(F32) + (got[0:96] + got[96:192]).reshape(3, 32, 256)
 
 
 def solution(mesh):
@@ -433,11 +445,18 @@
         dma = pltpu.SemaphoreType.DMA
         tile = (4, 3, 32, 256)
         strip = (3, 32, N)
-        out, r2, r3 = pl.pallas_call(
+        low_shape = jax.ShapeDtypeStruct((64, 640), BF)
+        base, low, *rest = pl.pallas_call(
             functools.partial(kernel, n_strip, n_lvl),
-            out_shape=(jax.ShapeDtypeStruct(strip, F32), jax.ShapeDtypeStruct(strip, BF), jax.ShapeDtypeStruct(strip, BF)),
+            out_shape=(
+                jax.ShapeDtypeStruct(strip, BF),
+                jax.ShapeDtypeStruct((64, 640), F32),
+                low_shape,
+                low_shape,
+                low_shape,
+            ),
             in_specs=[far] * (3 + len(NAMES)),
-            out_specs=(far, far, far),
+            out_specs=(far,) * 5,
             scratch_shapes=[
                 *[pltpu.VMEM(a.shape[1:] if name == "h35" else a.shape, a.dtype) for name, a in zip(NAMES, given)],
                 dma((len(NAMES) + 5,)),
@@ -450,21 +469,22 @@
                 pltpu.VMEM((512, 640), BF),
                 pltpu.VMEM((512, 640), BF),
                 pltpu.VMEM((512, 384), BF),
-                pltpu.VMEM((3, 256, N), BF),
-                pltpu.VMEM((192, 640), BF),
-                pltpu.VMEM((192, 640), BF),
-                pltpu.VMEM(tile, BF),
-                pltpu.VMEM(tile, BF),
-                pltpu.VMEM(tile, F32),
-                pltpu.VMEM(tile, BF),
-                pltpu.VMEM(tile, BF),
-                pltpu.VMEM(tile, F32),
-                dma((4,)),
-                dma((2,)), dma((2,)), dma((4,)), dma((4,)), dma((4,)), dma((4,)), dma((4,)), dma((4,)),
+                pltpu.VMEM((4, 384, 256), BF),
+                pltpu.VMEM((4, 384, 256), BF),
+                pltpu.VMEM((4, *tile), BF),
+                pltpu.VMEM((4, *tile), BF),
+                pltpu.VMEM(strip, BF),
+                pltpu.VMEM((3, 64, 640), BF),
+                pltpu.VMEM((64, 640), F32),
+                *[dma((2,))] * 3,
+                dma((4, 3)), dma((4, 3)), dma((3,)), dma((3,)),
             ],
             compiler_params=pltpu.CompilerParams(collective_id=0, has_side_effects=True),
         )(offsets, photos, seams, *given)
-        return out + (r2.astype(F32) + r3.astype(F32))
+        near = pl.BlockSpec(memory_space=pltpu.VMEM)
+        return pl.pallas_call(
+            finish, out_shape=jax.ShapeDtypeStruct(strip, F32), in_specs=[near] * 7, out_specs=near
+        )(base, low, *rest, jnp.asarray(table["e0"]), jnp.asarray(table["tall"]))
 
     placed = (P("strip", None, None, "lvl"), P("strip", None, None), P("strip"))
     return jax.shard_map(

time: 27.6 us -> 26 us (0.942)
  other arithmetic: 1.96 us -> 0 us
  Pallas kernels: 25.3 us -> 25.8 us
    pallas_call x0 -> x1, Pallas kernels: none -> 2.37 us  [per_device(): pl.pallas_call(finish, out_shape=jax.ShapeDtypeStruct(strip, F32), in_spe...]
    add x1 -> x0, other arithmetic: 1.96 us -> none  [per_device(): return out + (r2.astype(F32) + r3.astype(F32))]
    pallas_call x1, Pallas kernels: 25.3 us -> 23.5 us  [per_device(): pl.pallas_call(functools.partial(kernel, n_strip, n_lvl), out_shape=(jax....]
where the time goes in v4:
time: 26 us; the launch traced here: 25.9 us
  Pallas kernels  25.8 us (99%)
    pallas_call x1, Pallas kernels, per_device(): pl.pallas_call(functools.partial(kernel, n_strip, n_lvl), out_shape=(jax....  23.5 us
    pallas_call x1, Pallas kernels, per_device(): pl.pallas_call(finish, out_shape=jax.ShapeDtypeStruct(strip, F32), in_spe...  2.37 us

profile of v4, /device:TPU:2, one launch (start us, length us, event | category | flops | bytes accessed | tf_op | source)
XLA Modules:
  0.0 25.9 jit_solution(15740644362648035535)
XLA Ops:
  0.0 23.5 %shard_map.208 = (bf16[3,32,1024]{2,1,0:T(8,128)(2,1)}, f32[64,640]{1,0:T(8,128)}, bf16[64,640]{1,0:T(8,128)(2,1)}, bf16[64,640]{1,0:T(8,128)(2,1)}, bf16[64,640]{1,0:T(8,128)(2,1)}) custom-call(s32[4]{0:T(128)} %offsets_in.1, bf16[4,3,64,1024]{3,2,1,0:T(8,128)(2,1)} %photos_in.1, s32[4,2,64]{2,1,0:T(2,128)} %seams_in.1, ...), custom_call_target="tpu_custom_call" | custom-call | tf_op jit(solution)/shard_map/pallas_call | solution.py:449
  23.5 2.4 %shard_map.209 = f32[3,32,1024]{2,1,0:T(8,128)} custom-call(bf16[3,32,1024]{2,1,0:T(8,128)(2,1)} %get-tuple-element.10.base, f32[64,640]{1,0:T(8,128)} %get-tuple-element.11.low, bf16[64,640]{1,0:T(8,128)(2,1)} %get-tuple-element.12.q1, bf16[64,640]{1,0:T(8,128)(2,1)} %get-tuple-element.13.q2, bf16[64,640]{1,0:T(8,128)(2,1)} %get-tuple-element.14.q3, ...), custom_call_target="tpu_custom_call" | custom-call | tf_op jit(solution)/shard_map/pallas_call | solution.py:485

commit v5 on v4

--- a/solution.py
+++ b/solution.py
@@ -169,13 +169,13 @@
 
 def kernel(n_strip, n_lvl, offsets_in, photos_in, seams_in, *refs):
     n = len(NAMES)
-    given, outs, held, rest = refs[:n], refs[n : n + 5], refs[n + 5 : 2 * n + 5], refs[2 * n + 5 :]
+    given, outs, held, rest = refs[:n], refs[n : n + 9], refs[n + 9 : 2 * n + 9], refs[2 * n + 9 :]
     body(n_strip, n_lvl, offsets_in, photos_in, seams_in, dict(zip(NAMES, given)), *outs, dict(zip(NAMES, held)), *rest)
 
 
-def body(n_strip, n_lvl, offsets_in, photos_in, seams_in, given, base_out, own_out, q1, q2, q3, held, load, photos, offsets, seams, s0, s1, tm, g1,
-         ys, y2, uh, ul, sent, got_in, base, low, lowo, out_sem,
-         halo_send, halo_recv, m_send, m_recv, n_send, n_recv):
+def body(n_strip, n_lvl, offsets_in, photos_in, seams_in, given, base_out, own_out, late_out, q1, q2, q3, l1, l2, l3, held, load, photos, offsets, seams, s0, s1, tm, g1,
+         ys, y2, mk, uh, ul, sent, got_in, base, low, lowo, kept, late, lateo, out_sem,
+         halo_send, halo_recv, m_send, m_recv, n_send, n_recv, p_send, p_recv):
     x = lax.axis_index("strip")
     me = lax.axis_index("lvl")
     right, left = lax.rem(me + 1, n_lvl), lax.rem(me + n_lvl - 1, n_lvl)
@@ -202,8 +202,9 @@
 
     fetch("seams", seams_in, seams)
     fetch("v1", given["v1"], held["v1"])
-    for ch in range(3):
-        fetch(ch, photos_in.at[:, ch], photos.at[:, ch])
+    for name, at, width in (("west", 0, 128), ("east", N - 128, 128), ("middle", 128, N - 256)):
+        cols = slice(at, at + width)
+        fetch(name, photos_in.at[:, :, :, cols], photos.at[:, :, :, cols])
     fetch("offsets", offsets_in, offsets)
     for name in NAMES[1:]:
         fetch(name, given[name].at[edge] if name == "h35" else given[name], held[name])
@@ -212,8 +213,8 @@
         return photos[:, ch, :, start : start + width].reshape(256, width)
 
     lead = const("v1")[...]
-    for ch in range(3):
-        ready(ch)
+    ready("west")
+    ready("east")
     for start in (0, N - 128):
         for ch in range(3):
             tm[ch, :, HALO + start : HALO + start + 128] = dot(lead, rows_of(ch, start, 128)).astype(BF)
@@ -247,24 +248,26 @@
         a, b = s0[...], s1[...]
         return jnp.concatenate([(c >= a) & (c < b) for c in (col, col + 128.0)], axis=1)
 
+    for start in range(0, N + 256, 256):
+        m = jnp.where(mask_tile(start), 1.0, 0.0).astype(BF)
+        mk[:, start : start + 256] = m
+        tm[3, :, start : start + 256] = dot(lead, m).astype(BF)
+    ready("middle")
     for ch in range(3):
         tm[ch, :, 256 : N] = dot(lead, rows_of(ch, 128, N - 256)).astype(BF)
-    for start in range(0, N + 256, 256):
-        m = jnp.where(mask_tile(start), 1.0, 0.0).astype(BF)
-        tm[3, :, start : start + 256] = dot(lead, m).astype(BF)
 
     wred = const("wred")
 
-    def g1_tile(j):
+    def g1_tile(j, lo=0, hi=4):
         a, b = max(0, 2 * j - 1), min(10, 2 * j + 3)
         w = wred[128 * (a - 2 * j + 1) : 128 * (b - 2 * j + 1), :]
-        val = dot(tm[:, :, 128 * a : 128 * b].reshape(512, 128 * (b - a)), w)
+        val = dot(tm[lo:hi, :, 128 * a : 128 * b].reshape(128 * (hi - lo), 128 * (b - a)), w)
         if j in (0, 4):
             col = lax.broadcasted_iota(jnp.int32, (1, 128), 1) + (128 * j - 64) + me * (N // 2)
             val = jnp.where((col >= 0) & (col < n_lvl * (N // 2)), val, 0.0)
-        g1[:, 128 * j : 128 * j + 128] = val.astype(BF)
-
-    for j in (1, 2, 3):
+        g1[128 * lo : 128 * hi, 128 * j : 128 * j + 128] = val.astype(BF)
+
+    for j in (1, 2):
         g1_tile(j)
     e0, d0 = const("e0"), const("d0")
     ready("offsets")
@@ -292,73 +295,55 @@
         r = slice(128 * ch, 128 * ch + 128)
         away = dot(d0[...], jnp.concatenate([uh[t, r], ul[t, r]], axis=0))
         detail = rows_of(ch, 256 * t, 256).astype(F32) - away
-        weighted_0 = jnp.where(mask_tile(HALO + 256 * t), detail, 0.0).astype(BF)
+        weighted_0 = detail.astype(BF) * mk[:, HALO + 256 * t : HALO + 256 * t + 256]
+        if t in (0, 3):
+            kept[t // 3, ch] = weighted_0
+            return
         got = dot(put, weighted_0).astype(BF)
         for j in range(4):
-            sent[t, j, ch] = got[32 * j : 32 * j + 32]
+            sent[t - 1, j, ch] = got[32 * j : 32 * j + 32]
 
     def send_band(t):
         for j in (2, 1, 3):
-            sends.append(remote(sent.at[t, j], got_in.at[t, j], m_send.at[t, j - 1], m_recv.at[t, j - 1], others[j]))
-
-    widened(1)
-    widened(2)
+            k = j - 1
+            sends.append(remote(sent.at[t - 1, j], got_in.at[t - 1, j], m_send.at[t - 1, k], m_recv.at[t - 1, k], others[j]))
+
     for t in (1, 2):
+        if t == 2:
+            g1_tile(3)
+        widened(t)
         for ch in range(3):
             band(t, ch)
         send_band(t)
     for name in NAMES:
         ready(name)
-    for copy in halo:
-        copy.wait()
-    for at, outer in ((0, 0), (N + 128, n_lvl - 1)):
-        tm[0:3, :, at : at + 128] = jnp.where(me == outer, jnp.zeros((), BF), tm[0:3, :, at : at + 128])
+    col2 = lax.broadcasted_iota(jnp.int32, (1, 384), 1) - 32 + me * (N // 4)
+    inside2 = (col2 >= 0) & (col2 < n_lvl * (N // 4))
+
+    def deep(lo, hi):
+        count = hi - lo
+        rows = slice(128 * lo, 128 * hi)
+        for ch in range(lo, hi):
+            ys[128 * ch : 128 * ch + 128, :] = dot(held["v25"][...], g1[128 * ch : 128 * ch + 128, :]).astype(BF)
+        for j, a, b in ((0, 0, 3), (1, 1, 5), (2, 3, 5)):
+            w = wred[128 * (a - 2 * j + 1) : 128 * (b - 2 * j + 1), :]
+            val = dot(ys[rows, 128 * a : 128 * b], w)
+            y2[rows, 128 * j : 128 * j + 128] = jnp.where(inside2[:, 128 * j : 128 * j + 128], val, 0.0).astype(BF)
+        y = y2[rows, :].reshape(count, 128, 384)
+        y35 = dot(y[:, 64:128].reshape(64 * count, 384), held["h35"][...]).astype(BF).reshape(count, 64, 384)
+        return {
+            1: g1[rows, :],
+            2: y[:, 0:64].reshape(64 * count, 384),
+            3: y35[:, 0:32, 0:256].reshape(32 * count, 256),
+            4: y35[:, 32:48, 256:384].reshape(16 * count, 128),
+            5: y35[:, 48:64, 256:384].reshape(16 * count, 128),
+        }
+
     for j in (0, 4):
-        g1_tile(j)
-    widened(0)
-    widened(3)
-
-    for ch in range(4):
-        ys[128 * ch : 128 * ch + 128, :] = dot(const("v25")[...], g1[128 * ch : 128 * ch + 128, :]).astype(BF)
-    col = lax.broadcasted_iota(jnp.int32, (1, 384), 1) - 32 + me * (N // 4)
-    inside = (col >= 0) & (col < n_lvl * (N // 4))
-    for j, a, b in ((0, 0, 3), (1, 1, 5), (2, 3, 5)):
-        w = wred[128 * (a - 2 * j + 1) : 128 * (b - 2 * j + 1), :]
-        val = dot(ys[:, 128 * a : 128 * b], w)
-        y2[:, 128 * j : 128 * j + 128] = jnp.where(inside[:, 128 * j : 128 * j + 128], val, 0.0).astype(BF)
-    band(0, 0)
-    y = y2[...].reshape(4, 128, 384)
-    g2 = y[:, 0:64].reshape(256, 384)
-    y35 = dot(y[:, 64:128].reshape(256, 384), const("h35")[...]).astype(BF).reshape(4, 64, 384)
-    g3 = y35[:, 0:32, 0:256].reshape(128, 256)
-    g4 = y35[:, 32:48, 256:384].reshape(64, 128)
-    g5 = y35[:, 48:64, 256:384].reshape(64, 128)
-    band(0, 1)
-    gs = {1: g1[...], 2: g2, 3: g3, 4: g4, 5: g5}
-
-    weighted = {}
-    er = {k: const(f"er{k}") for k in (1, 2, 3, 4)}
-
-    def widen(k, field):
-        if k == 1:
-            return jnp.concatenate([dot(field[:, 0:256], held["ec1a"][...]), dot(field[:, 128:384], held["ec1b"][...])], axis=1)
-        return dot(field, held[f"ec{k}"][...])
-
-    for k, color in ((4, 48), (3, 48), (2, 96), (1, 192)):
-        tall = 4 * ROWS[k]
-        u_hi, u_lo = halves(dot(er[k][...], gs[k + 1][0:color]))
-        expanded = widen(k, jnp.concatenate([u_hi, u_lo], axis=0))
-        half = 3 * tall
-        g = gs[k].astype(F32)
-        detail = g[0:half] - (expanded[0:half] + expanded[half:])
-        m = g[half:]
-        weighted[k] = [(m * detail[ch * tall : ch * tall + tall]).astype(BF) for ch in range(3)]
-    band(0, 2)
-    send_band(0)
-    g = g5.astype(F32)
-    weighted[5] = [(g[48:64] * g[16 * ch : 16 * ch + 16]).astype(BF) for ch in range(3)]
-
-    pm, lb, lb5 = const("pm"), const("lb"), const("lb5")
+        g1_tile(j, 3, 4)
+    ms = deep(3, 4)
+
+    pm, lb, lb5 = held["pm"], held["lb"], held["lb5"]
 
     def by_photo(which):
         got = jnp.zeros(which.shape, F32)
@@ -369,6 +354,50 @@
     spot = by_photo(pm[0:1, :])
     table = sum(jnp.where(spot == float(o), lb[o].astype(F32), 0.0) for o in range(3)).astype(BF)
     fine = sum(jnp.where(spot[:, 384:] == float(o), lb5[o].astype(F32), 0.0) for o in range(3)).astype(BF)
+    q = lax.broadcasted_iota(jnp.int32, (128, 128), 0)
+    row = (((q >> 5) + x) & 3) * 32 + (q & 31)
+    d = (lax.broadcasted_iota(jnp.int32, (128, 128), 1) & 63) - (row >> 1)
+    even = jnp.where(d == 0, 0.75, jnp.where((d == 1) | (d == -1), 0.125, 0.0))
+    odd = jnp.where((d == 0) | (d == 1), 0.5, 0.0)
+    last = jnp.concatenate([put, jnp.where((row & 1) == 0, even, odd).astype(BF)], axis=1)
+
+    q = lax.broadcasted_iota(jnp.int32, (256, 192), 0)
+    k = lax.broadcasted_iota(jnp.int32, (256, 192), 1)
+    rest = q & 63
+    chan = jnp.where(rest >= 18, 1, 0) + jnp.where(rest >= 36, 1, 0)
+    row = (((q >> 6) + x) & 3) * 16 + rest - 18 * chan - 1
+    pick = jnp.where((rest < 54) & (row == (k & 63)) & (chan == (k >> 6)), 1.0, 0.0).astype(BF)
+    for copy in halo:
+        copy.wait()
+    for at, outer in ((0, 0), (N + 128, n_lvl - 1)):
+        tm[0:3, :, at : at + 128] = jnp.where(me == outer, jnp.zeros((), BF), tm[0:3, :, at : at + 128])
+    for t in (0, 3):
+        g1_tile(0 if t == 0 else 4, 0, 3)
+        widened(t)
+
+    gs = deep(0, 3)
+    band(0, 0)
+    band(0, 1)
+
+    weighted = {}
+    er = {k: const(f"er{k}") for k in (1, 2, 3, 4)}
+
+    def widen(k, field):
+        if k == 1:
+            return jnp.concatenate([dot(field[:, 0:256], held["ec1a"][...]), dot(field[:, 128:384], held["ec1b"][...])], axis=1)
+        return dot(field, held[f"ec{k}"][...])
+
+    for k, color in ((4, 48), (3, 48), (2, 96), (1, 192)):
+        tall = 4 * ROWS[k]
+        rough = dot(er[k][...], gs[k + 1][0:color])
+        expanded = widen(k, jnp.concatenate(halves(rough), axis=0))
+        expanded = expanded[: 3 * tall] + expanded[3 * tall :]
+        m = ms[k].astype(F32)
+        detail = gs[k].astype(F32) - expanded
+        weighted[k] = [(m * detail[ch * tall : ch * tall + tall]).astype(BF) for ch in range(3)]
+    weighted[5] = [(ms[5].astype(F32) * gs[5][16 * ch : 16 * ch + 16].astype(F32)).astype(BF) for ch in range(3)]
+
+    band(0, 2)
     band(3, 0)
     placed = {}
     for k in (5, 4, 3, 2, 1):
@@ -383,7 +412,6 @@
             parts.append(got[0:64] + got[64:128] if k >= 4 else got)
         placed[k] = jnp.concatenate(parts, axis=0)
 
-    band(3, 1)
     total = placed[5]
     for k in (4, 3, 2, 1):
         hi, lo = halves(total)
@@ -391,31 +419,38 @@
         col = lax.broadcasted_iota(jnp.int32, (1, PAD[k]), 1) - (HALO >> k) + me * (N >> k)
         ok = (col >= 0) & (col < n_lvl * (N >> k))
         total = placed[k] + jnp.where(ok, got[0:192] + got[192:384], 0.0)
-        if k == 4:
-            band(3, 2)
-            send_band(3)
-    q = lax.broadcasted_iota(jnp.int32, (256, 192), 0)
-    k = lax.broadcasted_iota(jnp.int32, (256, 192), 1)
-    rest = q & 63
-    ch = jnp.where(rest >= 18, 1, 0) + jnp.where(rest >= 36, 1, 0)
-    row = (((q >> 6) + x) & 3) * 16 + rest - 18 * ch - 1
-    pick = jnp.where((rest < 54) & (row == (k & 63)) & (ch == (k >> 6)), 1.0, 0.0).astype(BF)
+        if k in (4, 3):
+            band(3, 5 - k)
     hi, lo = halves(total)
-    got = dot(pick, hi)
+    got = dot(pick, hi[:, 128:512])
     lows = []
     for j, there in ((2, q2), (1, q1), (3, q3)):
         low[j - 1] = got[64 * j : 64 * j + 64].astype(BF)
         lows.append(remote(low.at[j - 1], there, n_send.at[j - 1], n_recv.at[j - 1], others[j]))
-    lowo[...] = got[0:64] + dot(pick[0:64], lo)
+    lowo[...] = got[0:64] + dot(pick[0:64], lo[:, 128:512])
     copies = [pltpu.make_async_copy(lowo, own_out, out_sem.at[0])]
     copies[0].start()
+    for i, t in ((0, 0), (1, 3)):
+        cols = slice(128 * t, 128 * t + 256)
+        wide = dot(jnp.concatenate([hi[:, cols], lo[:, cols]], axis=0), e0[...])
+        b_hi, b_lo = halves(wide[0:192] + wide[192:384])
+        for ch in range(3):
+            r = slice(64 * ch, 64 * ch + 64)
+            got = dot(last, jnp.concatenate([kept[i, ch], b_hi[r], b_lo[r]], axis=0))
+            lateo[i, ch] = got[0:32]
+            for j in (1, 2, 3):
+                late[i, j - 1, ch] = got[32 * j : 32 * j + 32].astype(BF)
+        for j, there in ((2, l2), (1, l1), (3, l3)):
+            lows.append(remote(late.at[i, j - 1], there.at[i], p_send.at[i, j - 1], p_recv.at[i, j - 1], others[j]))
+    copies.append(pltpu.make_async_copy(lateo, late_out, out_sem.at[2]))
+    copies[1].start()
 
     for copy in sends:
         copy.wait_recv()
-    for t in range(4):
+    for t in range(2):
         base[:, :, 256 * t : 256 * t + 256] = (sent[t, 0] + got_in[t, 1]) + (got_in[t, 2] + got_in[t, 3])
     copies.append(pltpu.make_async_copy(base, base_out, out_sem.at[1]))
-    copies[1].start()
+    copies[2].start()
     for copy in sends:
         copy.wait_send()
     for copy in lows:
@@ -424,15 +459,17 @@
         copy.wait()
 
 
-def finish(base, low, q1, q2, q3, e0, tall, out):
+def finish(base, low, late, q1, q2, q3, l1, l2, l3, e0, tall, out):
+    for i, t in ((0, 0), (1, 3)):
+        out[:, :, 256 * t : 256 * t + 256] = late[i] + (l2[i].astype(F32) + (l1[i].astype(F32) + l3[i].astype(F32)))
     total = low[...] + (q2[...].astype(F32) + (q1[...].astype(F32) + q3[...].astype(F32)))
     hi, lo = halves(total)
     hi, lo = halves(dot(tall[...], jnp.concatenate([hi, lo], axis=0)))
-    for t in range(4):
+    for t in (0, 1):
         cols = slice(128 * t, 128 * t + 256)
         got = dot(jnp.concatenate([hi[:, cols], lo[:, cols]], axis=0), e0[...])
         cols = slice(256 * t, 256 * t + 256)
-        out[:, :, cols] = base[:, :, cols].astype(F32) + (got[0:96] + got[96:192]).reshape(3, 32, 256)
+        out[:, :, 256 + 256 * t : 512 + 256 * t] = base[:, :, cols].astype(F32) + (got[0:96] + got[96:192]).reshape(3, 32, 256)
 
 
 def solution(mesh):
@@ -445,18 +482,19 @@
         dma = pltpu.SemaphoreType.DMA
         tile = (4, 3, 32, 256)
         strip = (3, 32, N)
-        low_shape = jax.ShapeDtypeStruct((64, 640), BF)
-        base, low, *rest = pl.pallas_call(
+        low_shape = jax.ShapeDtypeStruct((64, 384), BF)
+        late_shape = jax.ShapeDtypeStruct((2, 3, 32, 256), BF)
+        results = pl.pallas_call(
             functools.partial(kernel, n_strip, n_lvl),
             out_shape=(
-                jax.ShapeDtypeStruct(strip, BF),
-                jax.ShapeDtypeStruct((64, 640), F32),
-                low_shape,
-                low_shape,
-                low_shape,
+                jax.ShapeDtypeStruct((3, 32, 512), BF),
+                jax.ShapeDtypeStruct((64, 384), F32),
+                jax.ShapeDtypeStruct((2, 3, 32, 256), F32),
+                *[low_shape] * 3,
+                *[late_shape] * 3,
             ),
             in_specs=[far] * (3 + len(NAMES)),
-            out_specs=(far,) * 5,
+            out_specs=(far,) * 9,
             scratch_shapes=[
                 *[pltpu.VMEM(a.shape[1:] if name == "h35" else a.shape, a.dtype) for name, a in zip(NAMES, given)],
                 dma((len(NAMES) + 5,)),
@@ -469,22 +507,27 @@
                 pltpu.VMEM((512, 640), BF),
                 pltpu.VMEM((512, 640), BF),
                 pltpu.VMEM((512, 384), BF),
+                pltpu.VMEM((256, 1280), BF),
                 pltpu.VMEM((4, 384, 256), BF),
                 pltpu.VMEM((4, 384, 256), BF),
-                pltpu.VMEM((4, *tile), BF),
-                pltpu.VMEM((4, *tile), BF),
-                pltpu.VMEM(strip, BF),
-                pltpu.VMEM((3, 64, 640), BF),
-                pltpu.VMEM((64, 640), F32),
-                *[dma((2,))] * 3,
-                dma((4, 3)), dma((4, 3)), dma((3,)), dma((3,)),
+                pltpu.VMEM((2, *tile), BF),
+                pltpu.VMEM((2, *tile), BF),
+                pltpu.VMEM((3, 32, 512), BF),
+                pltpu.VMEM((3, 64, 384), BF),
+                pltpu.VMEM((64, 384), F32),
+                pltpu.VMEM((2, 3, 256, 256), BF),
+                pltpu.VMEM((2, 3, 3, 32, 256), BF),
+                pltpu.VMEM((2, 3, 32, 256), F32),
+                dma((3,)),
+                *[dma((2,))] * 2,
+                dma((2, 3)), dma((2, 3)), dma((3,)), dma((3,)), dma((2, 3)), dma((2, 3)),
             ],
             compiler_params=pltpu.CompilerParams(collective_id=0, has_side_effects=True),
         )(offsets, photos, seams, *given)
         near = pl.BlockSpec(memory_space=pltpu.VMEM)
         return pl.pallas_call(
-            finish, out_shape=jax.ShapeDtypeStruct(strip, F32), in_specs=[near] * 7, out_specs=near
-        )(base, low, *rest, jnp.asarray(table["e0"]), jnp.asarray(table["tall"]))
+            finish, out_shape=jax.ShapeDtypeStruct(strip, F32), in_specs=[near] * 11, out_specs=near
+        )(*results, jnp.asarray(table["e0"]), jnp.asarray(table["tall"]))
 
     placed = (P("strip", None, None, "lvl"), P("strip", None, None), P("strip"))
     return jax.shard_map(

time: 26 us -> 24.6 us (0.946)
  Pallas kernels: 25.8 us -> 24.5 us
    pallas_call x1, Pallas kernels: 23.5 us -> 22.2 us  [per_device(): pl.pallas_call(functools.partial(kernel, n_strip, n_lvl), out_shape=(jax....]
where the time goes in v5:
time: 24.6 us; the launch traced here: 24.5 us
  Pallas kernels  24.5 us (100%)
    pallas_call x1, Pallas kernels, per_device(): pl.pallas_call(functools.partial(kernel, n_strip, n_lvl), out_shape=(jax....  22.2 us
    pallas_call x1, Pallas kernels, per_device(): pl.pallas_call(finish, out_shape=jax.ShapeDtypeStruct(strip, F32), in_spe...  2.36 us

profile of v5, /device:TPU:2, one launch (start us, length us, event | category | flops | bytes accessed | tf_op | source)
XLA Modules:
  0.0 24.5 jit_solution(3643683672343695648)
XLA Ops:
  0.0 22.2 %shard_map.208 = (bf16[3,32,512]{2,1,0:T(8,128)(2,1)}, f32[64,384]{1,0:T(8,128)}, f32[2,3,32,256]{3,2,1,0:T(8,128)}, bf16[64,384]{1,0:T(8,128)(2,1)}, bf16[64,38...) custom-call(s32[4]{0:T(128)} %offsets_in.1, ...), custom_call_target="tpu_custom_call" | custom-call | tf_op jit(solution)/shard_map/pallas_call | solution.py:487
  22.2 2.4 %shard_map.209 = f32[3,32,1024]{2,1,0:T(8,128)} custom-call(bf16[3,32,512]{2,1,0:T(8,128)(2,1)} %get-tuple-element.14.base, f32[64,384]{1,0:T(8,128)} %get-tuple-element.15.low, f32[2,3,32,256]{3,2,1,0:T(8,128)} %get-tuple-element.16.late, bf16[64,384]{1,0:T(8,128)(2,1)} %get-tuple-element.17.q1, bf16[64,384]{1,0:T(8,128)(2,1)} %get-tuple-element.18.q2, ...), custom_call_target="tpu_custom_call" | custom-call | tf_op jit(solution)/shard_map/pallas_call | solution.py:528

commit v6 on v5

--- a/solution.py
+++ b/solution.py
@@ -218,6 +218,27 @@
     for start in (0, N - 128):
         for ch in range(3):
             tm[ch, :, HALO + start : HALO + start + 128] = dot(lead, rows_of(ch, start, 128)).astype(BF)
+    r_i = lax.broadcasted_iota(jnp.int32, (64, 64), 0)
+    c_i = lax.broadcasted_iota(jnp.int32, (64, 64), 1)
+    eye = r_i == c_i
+    ready("seams")
+    for p in range(4):
+        for e, dst in ((0, s0), (1, s1)):
+            line = seams[p, e : e + 1, :].astype(F32)
+            col = jnp.sum(jnp.where(eye, line, 0.0), axis=1, keepdims=True)
+            dst[64 * p : 64 * p + 64, :] = jnp.broadcast_to(col, (64, 128))
+
+    first_col = (me * N).astype(F32)
+
+    def mask_tile(start):
+        col = lax.broadcasted_iota(jnp.int32, (256, 128), 1).astype(F32) + (first_col + (start - HALO))
+        a, b = s0[...], s1[...]
+        return jnp.concatenate([(c >= a) & (c < b) for c in (col, col + 128.0)], axis=1)
+
+    for start in range(0, N + 256, 256):
+        m = jnp.where(mask_tile(start), 1.0, 0.0).astype(BF)
+        mk[:, start : start + 256] = m
+        tm[3, :, start : start + 256] = dot(lead, m).astype(BF)
     pl.semaphore_wait(barrier, 5)
     halo = []
     for i, (src, dst, target) in enumerate(((HALO, HALO + N, left), (N, 0, right))):
@@ -231,27 +252,6 @@
         )
         copy.start()
         halo.append(copy)
-    r_i = lax.broadcasted_iota(jnp.int32, (64, 64), 0)
-    c_i = lax.broadcasted_iota(jnp.int32, (64, 64), 1)
-    eye = r_i == c_i
-    ready("seams")
-    for p in range(4):
-        for e, dst in ((0, s0), (1, s1)):
-            line = seams[p, e : e + 1, :].astype(F32)
-            col = jnp.sum(jnp.where(eye, line, 0.0), axis=1, keepdims=True)
-            dst[64 * p : 64 * p + 64, :] = jnp.broadcast_to(col, (64, 128))
-
-    first_col = (me * N).astype(F32)
-
-    def mask_tile(start):
-        col = lax.broadcasted_iota(jnp.int32, (256, 128), 1).astype(F32) + (first_col + (start - HALO))
-        a, b = s0[...], s1[...]
-        return jnp.concatenate([(c >= a) & (c < b) for c in (col, col + 128.0)], axis=1)
-
-    for start in range(0, N + 256, 256):
-        m = jnp.where(mask_tile(start), 1.0, 0.0).astype(BF)
-        mk[:, start : start + 256] = m
-        tm[3, :, start : start + 256] = dot(lead, m).astype(BF)
     ready("middle")
     for ch in range(3):
         tm[ch, :, 256 : N] = dot(lead, rows_of(ch, 128, N - 256)).astype(BF)
@@ -296,10 +296,10 @@
         away = dot(d0[...], jnp.concatenate([uh[t, r], ul[t, r]], axis=0))
         detail = rows_of(ch, 256 * t, 256).astype(F32) - away
         weighted_0 = detail.astype(BF) * mk[:, HALO + 256 * t : HALO + 256 * t + 256]
-        if t in (0, 3):
-            kept[t // 3, ch] = weighted_0
-            return
-        got = dot(put, weighted_0).astype(BF)
+        kept[t, ch] = weighted_0
+
+    def place(t, ch):
+        got = dot(put, kept[t, ch]).astype(BF)
         for j in range(4):
             sent[t - 1, j, ch] = got[32 * j : 32 * j + 32]
 
@@ -308,15 +308,6 @@
             k = j - 1
             sends.append(remote(sent.at[t - 1, j], got_in.at[t - 1, j], m_send.at[t - 1, k], m_recv.at[t - 1, k], others[j]))
 
-    for t in (1, 2):
-        if t == 2:
-            g1_tile(3)
-        widened(t)
-        for ch in range(3):
-            band(t, ch)
-        send_band(t)
-    for name in NAMES:
-        ready(name)
     col2 = lax.broadcasted_iota(jnp.int32, (1, 384), 1) - 32 + me * (N // 4)
     inside2 = (col2 >= 0) & (col2 < n_lvl * (N // 4))
 
@@ -325,13 +316,15 @@
         rows = slice(128 * lo, 128 * hi)
         for ch in range(lo, hi):
             ys[128 * ch : 128 * ch + 128, :] = dot(held["v25"][...], g1[128 * ch : 128 * ch + 128, :]).astype(BF)
+        yield
         for j, a, b in ((0, 0, 3), (1, 1, 5), (2, 3, 5)):
             w = wred[128 * (a - 2 * j + 1) : 128 * (b - 2 * j + 1), :]
             val = dot(ys[rows, 128 * a : 128 * b], w)
             y2[rows, 128 * j : 128 * j + 128] = jnp.where(inside2[:, 128 * j : 128 * j + 128], val, 0.0).astype(BF)
+        yield
         y = y2[rows, :].reshape(count, 128, 384)
         y35 = dot(y[:, 64:128].reshape(64 * count, 384), held["h35"][...]).astype(BF).reshape(count, 64, 384)
-        return {
+        yield {
             1: g1[rows, :],
             2: y[:, 0:64].reshape(64 * count, 384),
             3: y35[:, 0:32, 0:256].reshape(32 * count, 256),
@@ -339,10 +332,25 @@
             5: y35[:, 48:64, 256:384].reshape(16 * count, 128),
         }
 
-    for j in (0, 4):
-        g1_tile(j, 3, 4)
-    ms = deep(3, 4)
-
+    g1_tile(3)
+    widened(1)
+    widened(2)
+    band(1, 0)
+    band(1, 1)
+    place(1, 0)
+    band(1, 2)
+    place(1, 1)
+    place(1, 2)
+    send_band(1)
+    band(2, 0)
+    band(2, 1)
+    place(2, 0)
+    band(2, 2)
+    place(2, 1)
+    place(2, 2)
+    send_band(2)
+    for name in NAMES:
+        ready(name)
     pm, lb, lb5 = held["pm"], held["lb"], held["lb5"]
 
     def by_photo(which):
@@ -372,12 +380,18 @@
     for at, outer in ((0, 0), (N + 128, n_lvl - 1)):
         tm[0:3, :, at : at + 128] = jnp.where(me == outer, jnp.zeros((), BF), tm[0:3, :, at : at + 128])
     for t in (0, 3):
-        g1_tile(0 if t == 0 else 4, 0, 3)
+        g1_tile(0 if t == 0 else 4)
         widened(t)
 
-    gs = deep(0, 3)
+    colors, masks = deep(0, 3), deep(3, 4)
+    next(colors)
+    next(masks)
     band(0, 0)
+    next(colors)
+    next(masks)
     band(0, 1)
+    gs = next(colors)
+    ms = next(masks)
 
     weighted = {}
     er = {k: const(f"er{k}") for k in (1, 2, 3, 4)}
@@ -430,13 +444,16 @@
     lowo[...] = got[0:64] + dot(pick[0:64], lo[:, 128:512])
     copies = [pltpu.make_async_copy(lowo, own_out, out_sem.at[0])]
     copies[0].start()
-    for i, t in ((0, 0), (1, 3)):
+    grown = []
+    for t in (0, 3):
         cols = slice(128 * t, 128 * t + 256)
         wide = dot(jnp.concatenate([hi[:, cols], lo[:, cols]], axis=0), e0[...])
-        b_hi, b_lo = halves(wide[0:192] + wide[192:384])
+        grown.append(halves(wide[0:192] + wide[192:384]))
+    for i, t in ((0, 0), (1, 3)):
+        b_hi, b_lo = grown[i]
         for ch in range(3):
             r = slice(64 * ch, 64 * ch + 64)
-            got = dot(last, jnp.concatenate([kept[i, ch], b_hi[r], b_lo[r]], axis=0))
+            got = dot(last, jnp.concatenate([kept[t, ch], b_hi[r], b_lo[r]], axis=0))
             lateo[i, ch] = got[0:32]
             for j in (1, 2, 3):
                 late[i, j - 1, ch] = got[32 * j : 32 * j + 32].astype(BF)
@@ -515,7 +532,7 @@
                 pltpu.VMEM((3, 32, 512), BF),
                 pltpu.VMEM((3, 64, 384), BF),
                 pltpu.VMEM((64, 384), F32),
-                pltpu.VMEM((2, 3, 256, 256), BF),
+                pltpu.VMEM((4, 3, 256, 256), BF),
                 pltpu.VMEM((2, 3, 3, 32, 256), BF),
                 pltpu.VMEM((2, 3, 32, 256), F32),
                 dma((3,)),

time: 24.6 us -> 24.6 us (level)
  no operation moved by 1% of the time
where the time goes in v6:
time: 24.6 us; the launch traced here: 24.5 us
  Pallas kernels  24.5 us (100%)
    pallas_call x1, Pallas kernels, per_device(): pl.pallas_call(functools.partial(kernel, n_strip, n_lvl), out_shape=(jax....  22.2 us
    pallas_call x1, Pallas kernels, per_device(): pl.pallas_call(finish, out_shape=jax.ShapeDtypeStruct(strip, F32), in_spe...  2.36 us

profile of v6, /device:TPU:2, one launch (start us, length us, event | category | flops | bytes accessed | tf_op | source)
XLA Modules:
  0.0 24.5 jit_solution(6260394100498973213)
XLA Ops:
  0.0 22.2 %shard_map.208 = (bf16[3,32,512]{2,1,0:T(8,128)(2,1)}, f32[64,384]{1,0:T(8,128)}, f32[2,3,32,256]{3,2,1,0:T(8,128)}, bf16[64,384]{1,0:T(8,128)(2,1)}, bf16[64,38...) custom-call(s32[4]{0:T(128)} %offsets_in.1, ...), custom_call_target="tpu_custom_call" | custom-call | tf_op jit(solution)/shard_map/pallas_call | solution.py:504
  22.2 2.4 %shard_map.209 = f32[3,32,1024]{2,1,0:T(8,128)} custom-call(bf16[3,32,512]{2,1,0:T(8,128)(2,1)} %get-tuple-element.14.base, f32[64,384]{1,0:T(8,128)} %get-tuple-element.15.low, f32[2,3,32,256]{3,2,1,0:T(8,128)} %get-tuple-element.16.late, bf16[64,384]{1,0:T(8,128)(2,1)} %get-tuple-element.17.q1, bf16[64,384]{1,0:T(8,128)(2,1)} %get-tuple-element.18.q2, ...), custom_call_target="tpu_custom_call" | custom-call | tf_op jit(solution)/shard_map/pallas_call | solution.py:545

commit v7 on v6

--- a/solution.py
+++ b/solution.py
@@ -444,13 +444,10 @@
     lowo[...] = got[0:64] + dot(pick[0:64], lo[:, 128:512])
     copies = [pltpu.make_async_copy(lowo, own_out, out_sem.at[0])]
     copies[0].start()
-    grown = []
-    for t in (0, 3):
+    for i, t in ((0, 0), (1, 3)):
         cols = slice(128 * t, 128 * t + 256)
         wide = dot(jnp.concatenate([hi[:, cols], lo[:, cols]], axis=0), e0[...])
-        grown.append(halves(wide[0:192] + wide[192:384]))
-    for i, t in ((0, 0), (1, 3)):
-        b_hi, b_lo = grown[i]
+        b_hi, b_lo = halves(wide[0:192] + wide[192:384])
         for ch in range(3):
             r = slice(64 * ch, 64 * ch + 64)
             got = dot(last, jnp.concatenate([kept[t, ch], b_hi[r], b_lo[r]], axis=0))

time: 24.6 us -> 24.6 us (level)
  no operation moved by 1% of the time
where the time goes in v7:
time: 24.6 us; the launch traced here: 24.5 us
  Pallas kernels  24.5 us (100%)
    pallas_call x1, Pallas kernels, per_device(): pl.pallas_call(functools.partial(kernel, n_strip, n_lvl), out_shape=(jax....  22.2 us
    pallas_call x1, Pallas kernels, per_device(): pl.pallas_call(finish, out_shape=jax.ShapeDtypeStruct(strip, F32), in_spe...  2.36 us

profile of v7, /device:TPU:2, one launch (start us, length us, event | category | flops | bytes accessed | tf_op | source)
XLA Modules:
  0.0 24.5 jit_solution(16442756254132579287)
XLA Ops:
  0.0 22.2 %shard_map.208 = (bf16[3,32,512]{2,1,0:T(8,128)(2,1)}, f32[64,384]{1,0:T(8,128)}, f32[2,3,32,256]{3,2,1,0:T(8,128)}, bf16[64,384]{1,0:T(8,128)(2,1)}, bf16[64,38...) custom-call(s32[4]{0:T(128)} %offsets_in.1, ...), custom_call_target="tpu_custom_call" | custom-call | tf_op jit(solution)/shard_map/pallas_call | solution.py:501
  22.2 2.4 %shard_map.209 = f32[3,32,1024]{2,1,0:T(8,128)} custom-call(bf16[3,32,512]{2,1,0:T(8,128)(2,1)} %get-tuple-element.14.base, f32[64,384]{1,0:T(8,128)} %get-tuple-element.15.low, f32[2,3,32,256]{3,2,1,0:T(8,128)} %get-tuple-element.16.late, bf16[64,384]{1,0:T(8,128)(2,1)} %get-tuple-element.17.q1, bf16[64,384]{1,0:T(8,128)(2,1)} %get-tuple-element.18.q2, ...), custom_call_target="tpu_custom_call" | custom-call | tf_op jit(solution)/shard_map/pallas_call | solution.py:542

commit v8 on v7

--- a/solution.py
+++ b/solution.py
@@ -441,9 +441,7 @@
     for j, there in ((2, q2), (1, q1), (3, q3)):
         low[j - 1] = got[64 * j : 64 * j + 64].astype(BF)
         lows.append(remote(low.at[j - 1], there, n_send.at[j - 1], n_recv.at[j - 1], others[j]))
-    lowo[...] = got[0:64] + dot(pick[0:64], lo[:, 128:512])
-    copies = [pltpu.make_async_copy(lowo, own_out, out_sem.at[0])]
-    copies[0].start()
+    lowo[...] = got[0:64]
     for i, t in ((0, 0), (1, 3)):
         cols = slice(128 * t, 128 * t + 256)
         wide = dot(jnp.concatenate([hi[:, cols], lo[:, cols]], axis=0), e0[...])
@@ -456,6 +454,9 @@
                 late[i, j - 1, ch] = got[32 * j : 32 * j + 32].astype(BF)
         for j, there in ((2, l2), (1, l1), (3, l3)):
             lows.append(remote(late.at[i, j - 1], there.at[i], p_send.at[i, j - 1], p_recv.at[i, j - 1], others[j]))
+    lowo[...] = lowo[...] + dot(pick[0:64], lo[:, 128:512])
+    copies = [pltpu.make_async_copy(lowo, own_out, out_sem.at[0])]
+    copies[0].start()
     copies.append(pltpu.make_async_copy(lateo, late_out, out_sem.at[2]))
     copies[1].start()
 

time: 24.6 us -> 24.6 us (level)
  no operation moved by 1% of the time
where the time goes in v8:
time: 24.6 us; the launch traced here: 24.5 us
  Pallas kernels  24.5 us (100%)
    pallas_call x1, Pallas kernels, per_device(): pl.pallas_call(functools.partial(kernel, n_strip, n_lvl), out_shape=(jax....  22.2 us
    pallas_call x1, Pallas kernels, per_device(): pl.pallas_call(finish, out_shape=jax.ShapeDtypeStruct(strip, F32), in_spe...  2.36 us

profile of v8, /device:TPU:2, one launch (start us, length us, event | category | flops | bytes accessed | tf_op | source)
XLA Modules:
  0.0 24.5 jit_solution(9221065001835032706)
XLA Ops:
  0.0 22.2 %shard_map.208 = (bf16[3,32,512]{2,1,0:T(8,128)(2,1)}, f32[64,384]{1,0:T(8,128)}, f32[2,3,32,256]{3,2,1,0:T(8,128)}, bf16[64,384]{1,0:T(8,128)(2,1)}, bf16[64,38...) custom-call(s32[4]{0:T(128)} %offsets_in.1, ...), custom_call_target="tpu_custom_call" | custom-call | tf_op jit(solution)/shard_map/pallas_call | solution.py:502
  22.2 2.4 %shard_map.209 = f32[3,32,1024]{2,1,0:T(8,128)} custom-call(bf16[3,32,512]{2,1,0:T(8,128)(2,1)} %get-tuple-element.14.base, f32[64,384]{1,0:T(8,128)} %get-tuple-element.15.low, f32[2,3,32,256]{3,2,1,0:T(8,128)} %get-tuple-element.16.late, bf16[64,384]{1,0:T(8,128)(2,1)} %get-tuple-element.17.q1, bf16[64,384]{1,0:T(8,128)(2,1)} %get-tuple-element.18.q2, ...), custom_call_target="tpu_custom_call" | custom-call | tf_op jit(solution)/shard_map/pallas_call | solution.py:543
